TPU v7x, 256 devices: a whole 4x4x8 slice. The times are simulated.
256 devices in a mesh: gx: 16 (over z_hi, y), gy: 4 (over x), sa: 4 (over z_lo, core).
Axes of the slice: x: 4, y: 4, z: 8 (z_hi: 4, z_lo: 2; z = z_hi * 2 + z_lo), core: 2. Of those that a mesh axis runs over, the one named last changes fastest.
Arguments:
- volume: bfloat16 [4, 128, 64, 256], P('sa', 'gx', 'gy'), may hold values from -6 to 6
- first_kernel: bfloat16 [27, 128], replicated, may hold values from -0.625 to 0.625
- second_kernel: bfloat16 [27, 2048], replicated, may hold values from -0.21875 to 0.21875
- cotangent: bfloat16 [4, 32, 16, 1024], P('sa', 'gx', 'gy'), may hold values from -0.14941406 to 0.14941406
Outputs:
- stem_output: bfloat16 [4, 32, 16, 1024], P('sa', 'gx', 'gy')
- first_weights: float32 [27, 128], replicated
- second_weights: float32 [27, 2048], replicated
All inputs are finite; a program needn't handle non-finite values.
Results may differ from a plain program's by a relative error of at most 0.0051.
Values may be sent and summed in bfloat16 or wider, within the bound.
A program may use at most 64 MiB of HBM per device.

v0:
```python
import jax
import jax.numpy as jnp
import numpy as np
from jax import lax
from jax.experimental import pallas as pl
from jax.experimental.pallas import tpu as pltpu
from jax.sharding import PartitionSpec as P

CH_IN = 4
CH_ONE = 32
CH_TWO = 64

MESH = pl.DeviceIdType.MESH
CHUNK = 32


def sum_kernel(x_ref, out_ref, near, part, far, gathered, sends, recvs):
    row = lax.axis_index("gx")
    column = lax.axis_index("gy")
    sample = lax.axis_index("sa")
    me = column * 4 + sample
    barrier = pltpu.get_barrier_semaphore()

    def plane_peer(k):
        other = (me + k) % 16
        return other, (row, other // 4, other % 4)

    def row_peer(k):
        other = (row + k) % 16
        return other, (other, column, sample)

    for k in range(1, 16):
        pl.semaphore_signal(barrier, inc=1, device_id=plane_peer(k)[1], device_id_type=MESH)
        pl.semaphore_signal(barrier, inc=1, device_id=row_peer(k)[1], device_id_type=MESH)
    pl.semaphore_wait(barrier, 30)

    def send(stage, k, source, target, device):
        copy = pltpu.make_async_remote_copy(
            src_ref=source,
            dst_ref=target,
            send_sem=sends.at[stage, k],
            recv_sem=recvs.at[stage, k],
            device_id=device,
            device_id_type=MESH,
        )
        copy.start()
        return copy

    copies = []
    for k in range(1, 16):
        other, device = plane_peer(k)
        copies.append(send(0, k, x_ref.at[other], near.at[k], device))
    total = x_ref[me]
    for k in range(1, 16):
        copies[k - 1].wait_recv()
        total = total + near[k]
    part[...] = total
    far[row] = total
    second = []
    for k in range(1, 16):
        other, device = row_peer(k)
        second.append(send(1, k, part, far.at[row], device))
    for copy in second:
        copy.wait_recv()
    total = far[0]
    for k in range(1, 16):
        total = total + far[k]
    gathered[me] = total
    third = []
    for k in range(1, 16):
        other, device = plane_peer(k)
        third.append(send(2, k, gathered.at[me], gathered.at[me], device))
    for copy in third:
        copy.wait_recv()
    out_ref[...] = gathered[...]
    for copy in copies + second + third:
        copy.wait_send()


def sum_over_devices(first, second):
    filler = jnp.zeros((16 * CHUNK * 128 - first.size - second.size,), jnp.float32)
    flat = jnp.concatenate([second.reshape(-1), first.reshape(-1), filler])
    block = (16, CHUNK, 128)
    total = pl.pallas_call(
        sum_kernel,
        out_shape=jax.ShapeDtypeStruct(block, jnp.float32),
        in_specs=[pl.BlockSpec(memory_space=pltpu.VMEM)],
        out_specs=pl.BlockSpec(memory_space=pltpu.VMEM),
        scratch_shapes=[
            pltpu.VMEM(block, jnp.float32),
            pltpu.VMEM(block[1:], jnp.float32),
            pltpu.VMEM(block, jnp.float32),
            pltpu.VMEM(block, jnp.float32),
            pltpu.SemaphoreType.DMA((3, 16)),
            pltpu.SemaphoreType.DMA((3, 16)),
        ],
        compiler_params=pltpu.CompilerParams(collective_id=0, has_side_effects=True),
        name="sum_over_devices",
    )(flat.reshape(block)).reshape(-1)
    return (
        total[second.size : second.size + first.size].reshape(first.shape),
        total[: second.size].reshape(second.shape),
    )


def padded_2(x, sides, width):
    for axis, dim in sides:
        peers, length = (lax.axis_size(axis), x.shape[dim])
        up = [(i, (i + 1) % peers) for i in range(peers)]
        down = [(j, i) for i, j in up]
        last = lax.slice_in_dim(x, length - width, length, axis=dim)
        first = lax.slice_in_dim(x, 0, width, axis=dim)
        before = lax.ppermute(last, axis, up)
        after = lax.ppermute(first, axis, down)
        x = jnp.concatenate([before, x, after], axis=dim)
    return x


PLANES_ONE = 16
PLANES_TWO = 4


def band(planes, inputs, outputs):
    rows = np.arange((planes + 2) * inputs)
    half = planes // 2 * outputs
    columns = np.arange(2 * half)
    plane = 2 * (columns % half // outputs) + columns // half
    masks = [rows[:, None] // inputs - plane[None, :] == c for c in range(3)]
    spread_rows = rows[:, None] % inputs == np.arange(inputs)[None, :]
    spread_columns = np.arange(outputs)[:, None] == columns[None, :] % outputs
    return np.stack(masks), spread_rows, spread_columns


def banded(kernel, planes, inputs, outputs):
    masks, spread_rows, spread_columns = band(planes, inputs, outputs)
    wide = jnp.dot(
        kernel.reshape(27 * inputs, outputs),
        jnp.asarray(spread_columns, jnp.bfloat16),
        preferred_element_type=jnp.bfloat16,
    ).reshape(9, 3, inputs, -1)
    spread_rows = jnp.asarray(spread_rows, jnp.bfloat16)
    full = jnp.einsum("ri,kcin->kcrn", spread_rows, wide, preferred_element_type=jnp.bfloat16)
    full = jnp.where(masks[None], full, jnp.bfloat16(0)).sum(axis=1, dtype=jnp.bfloat16)
    return full.reshape(3, 3, full.shape[1], full.shape[2])


def unbanded(grad, planes, inputs, outputs):
    masks, spread_rows, spread_columns = band(planes, inputs, outputs)
    grad = grad.reshape(9, planes + 2, inputs, -1)
    masks = masks.reshape(3, planes + 2, inputs, -1)
    parts = [jnp.where(masks[c][None], grad, 0.0).sum(axis=1) for c in range(3)]
    narrow = jnp.stack(parts, axis=1).reshape(27 * inputs, -1)
    narrow = jnp.dot(
        narrow,
        jnp.asarray(spread_columns.T, jnp.float32),
        precision=lax.Precision.HIGHEST,
        preferred_element_type=jnp.float32,
    )
    return narrow.reshape(27, inputs * outputs)


def convolve(padded, weight, padding="VALID", form="HWIO"):
    return lax.conv_general_dilated(
        padded,
        weight,
        (1, 1),
        padding,
        dimension_numbers=("NHWC", form, "NHWC"),
        preferred_element_type=jnp.float32,
    )


def weight_gradient(padded, grad):
    return lax.conv_general_dilated(
        padded,
        grad,
        (1, 1),
        "VALID",
        dimension_numbers=("CHWN", "IHWO", "HWNC"),
        preferred_element_type=jnp.float32,
    )


def average_pool(values):
    batch, rows_x, rows_y, lanes = values.shape
    values = values[..., : lanes // 2] + values[..., lanes // 2 :]
    values = values.reshape(batch, rows_x // 2, 2, rows_y // 2, 2, lanes // 2)
    return values.sum(axis=(2, 4)) * 0.125


def upsample(values):
    values = jnp.repeat(jnp.repeat(values, 2, axis=1), 2, axis=2)
    return jnp.concatenate([values, values], axis=-1)


def chunks(values, width, margin, count):
    step = width - 2 * margin
    values = jnp.pad(values, ((0, 0), (0, 0), (margin, margin)))
    return jnp.stack([values[..., j * step : j * step + width] for j in range(count)])


def merge(values):
    return jnp.concatenate(list(values), axis=-1)


def silu_slope(values):
    sigma = jax.nn.sigmoid(values)
    return sigma * (1.0 + values * (1.0 - sigma))


def body(volume, first_kernel, second_kernel, cotangent):
    sides = (("gx", 0), ("gy", 1))
    weight_one = banded(first_kernel, PLANES_ONE, CH_IN, CH_ONE)
    weight_two = banded(second_kernel, PLANES_TWO, CH_ONE, CH_TWO)
    outer = padded_2(cotangent[0], sides, 1)
    fields = padded_2(volume[0], sides, 5)
    count = fields.shape[-1] // (PLANES_ONE * CH_IN)
    fields = chunks(fields, (PLANES_ONE + 2) * CH_IN, CH_IN, count)
    first_pre = convolve(fields, weight_one)
    pooled = merge(average_pool(jax.nn.silu(first_pre)).astype(jnp.bfloat16))
    pooled = chunks(pooled, (PLANES_TWO + 2) * CH_ONE, CH_ONE, 2 * count)
    second_pre = convolve(pooled, weight_two)
    inner = second_pre[:, 1:-1, 1:-1]
    result = merge(average_pool(jax.nn.silu(inner)).astype(jnp.bfloat16))
    outer = jnp.stack(jnp.split(outer, 2 * count, axis=-1))
    outer = upsample(outer)[:, 1:-1, 1:-1].astype(jnp.float32)
    second_grad = (outer * (0.125 * silu_slope(second_pre))).astype(jnp.bfloat16)
    grad_two = weight_gradient(pooled[:, 1:-1, 1:-1], second_grad[:, 1:-1, 1:-1])
    second_weights = unbanded(grad_two, PLANES_TWO, CH_ONE, CH_TWO)
    spread = convolve(second_grad, weight_two[::-1, ::-1], form="HWOI")
    middle = merge(spread[..., CH_ONE:-CH_ONE])
    below = jnp.pad(spread[1:, ..., :CH_ONE], ((0, 1), (0, 0), (0, 0), (0, 0)))
    above = jnp.pad(spread[:-1, ..., -CH_ONE:], ((1, 0), (0, 0), (0, 0), (0, 0)))
    room = ((0, 0), (0, 0), (0, 0))
    width = (PLANES_TWO - 1) * CH_ONE
    middle = middle + merge(jnp.pad(below, room + ((width, 0),)))
    middle = middle + merge(jnp.pad(above, room + ((0, width),)))
    pooled_grad = jnp.stack(jnp.split(middle, count, axis=-1))
    slope = 0.125 * silu_slope(first_pre[:, 4:-4, 4:-4])
    first_grad = (upsample(pooled_grad) * slope).astype(jnp.bfloat16)
    grad_one = weight_gradient(fields[:, 4:-4, 4:-4], first_grad)
    first_weights = unbanded(grad_one, PLANES_ONE, CH_IN, CH_ONE)
    first_weights, second_weights = sum_over_devices(first_weights, second_weights)
    return (result[None], first_weights, second_weights)


def solution(mesh):
    in_specs = (P("sa", "gx", "gy", None), P(), P(), P("sa", "gx", "gy", None))
    out_specs = (P("sa", "gx", "gy", None), P(), P())
    return jax.shard_map(body, mesh=mesh, in_specs=in_specs, out_specs=out_specs, check_vma=False)
```

profile of v0, /device:TPU:1, one launch (start us, length us, event | category | flops | bytes accessed | tf_op | source)
XLA Modules:
  0.0 90.4 jit_solution(9511434830558662060)
XLA Ops:
  0.6 0.9 slice_bitcast_fusion.5
  1.5 2.1 %collective-permute-start = (bf16[5,16,256]{2,1,0:T(8,128)(2,1)S(1)}, bf16[5,16,256]{2,1,0:T(8,128)(2,1)S(1)}, u32[]{:S(2)}, u32[]{:S(2)}) collective-permute-start(bf16[5,16,256]{2,1,0:T(8,128)(2,1)S(1)} %get-tuple-element.49), channel_id=1, source_target_pairs={{0,16},{16,32},{32,48},{48,64},{64,80},{80,96},{96,112},{112,128},... | collective-permute-start | bytes 122888 | tf_op jit(solution)/shard_map/ppermute | solution.py:113
  3.6 7.3 %collective-permute-start.1 = (bf16[5,16,256]{2,1,0:T(8,128)(2,1)S(1)}, bf16[5,16,256]{2,1,0:T(8,128)(2,1)S(1)}, u32[]{:S(2)}, u32[]{:S(2)}) collective-permute-start(bf16[5,16,256]{2,1,0:T(8,128)(2,1)S(1)} %get-tuple-element.50), channel_id=1, source_target_pairs={{16,0},{32,16},{48,32},{64,48},{80,64},{96,80},{112,96},{128,112},... | collective-permute-start | bytes 122888 | tf_op jit(solution)/shard_map/ppermute | solution.py:114
  10.9 0.7 slice_bitcast_fusion.19
  11.7 5.7 %collective-permute-start.5 = (bf16[1,4,1024]{2,1,0:T(4,128)(2,1)S(1)}, bf16[1,4,1024]{2,1,0:T(4,128)(2,1)S(1)}, u32[]{:S(2)}, u32[]{:S(2)}) collective-permute-start(bf16[1,4,1024]{2,1,0:T(4,128)(2,1)S(1)} %get-tuple-element.58), channel_id=1, source_target_pairs={{16,0},{32,16},{48,32},{64,48},{80,64},{96,80},{112,96},{128,112},... | collective-permute-start | bytes 24584 | tf_op jit(solution)/shard_map/ppermute | solution.py:114
  17.4 0.8 dot_general.22
  18.1 1.2 %dot_general.25 = bf16[9,3,32,64]{3,2,1,0:T(8,128)(2,1)S(1)} reshape(bf16[27,2048]{1,0:T(8,128)(2,1)} %param.20) | data formatting | bytes 221184 | tf_op jit(solution)/shard_map/dot_general | solution.py:136
  19.3 1.0 %copy.819 = pred[3,192,256]{2,1,0:T(8,128)(4,1)S(1)} copy(pred[3,192,256]{2,1,0:T(32,128)(4,1)} %constant.77) | data formatting | bytes 294912
  20.3 2.0 %fusion = bf16[9,192,256]{2,1,0:T(8,128)(2,1)S(1)} fusion(pred[3,192,256]{2,1,0:T(8,128)(4,1)S(1)} %copy.819, bf16[192,32,1,1]{0,1,3,2:T(8,128)(2,1)} %constant.87, bf16[64,256,1,1]{1,0,3,2:T(8,128)(2,1)} %constant.86, bf16[9,3,32,64]{3,2,1,0:T(8,128)(2,1)S(1)} %dot_general.25), kind=kOutput, calls=%fused_computation.2 | convolution fusion | flops 115458048 | bytes 1187840 | tf_op jit(solution)/shard_map/ri,kcin->kcrn/dot_general | solution.py:142
  22.6 1.3 %collective-permute-start.6 = (bf16[4,1,1024]{2,1,0:T(2,128)(2,1)S(1)}, bf16[4,1,1024]{2,1,0:T(2,128)(2,1)S(1)}, u32[]{:S(2)}, u32[]{:S(2)}) collective-permute-start(bf16[4,1,1024]{2,1,0:T(2,128)(2,1)S(1)} %get-tuple-element.55), channel_id=1, source_target_pairs={{0,4},{4,8},{8,12},{12,0},{1,5},{5,9},{9,13},{13,1},{2,6},{6,10},{... | collective-permute-start | bytes 24584 | tf_op jit(solution)/shard_map/ppermute | solution.py:113
  23.9 1.5 %collective-permute-start.7 = (bf16[4,1,1024]{2,1,0:T(2,128)(2,1)S(1)}, bf16[4,1,1024]{2,1,0:T(2,128)(2,1)S(1)}, u32[]{:S(2)}, u32[]{:S(2)}) collective-permute-start(bf16[4,1,1024]{2,1,0:T(2,128)(2,1)S(1)} %get-tuple-element.56), channel_id=1, source_target_pairs={{4,0},{8,4},{12,8},{0,12},{5,1},{9,5},{13,9},{1,13},{6,2},{10,6},{... | collective-permute-start | bytes 24584 | tf_op jit(solution)/shard_map/ppermute | solution.py:114
  25.4 0.8 fusion.1
  26.8 1.3 %collective-permute-start.2 = (bf16[18,5,256]{2,1,0:T(8,128)(2,1)S(1)}, bf16[18,5,256]{2,1,0:T(8,128)(2,1)S(1)}, u32[]{:S(2)}, u32[]{:S(2)}) collective-permute-start(bf16[18,5,256]{2,1,0:T(8,128)(2,1)S(1)} %get-tuple-element.29), channel_id=1, source_target_pairs={{0,4},{4,8},{8,12},{12,0},{1,5},{5,9},{9,13},{13,1},{2,6},{6,10},{... | collective-permute-start | bytes 138248 | tf_op jit(solution)/shard_map/ppermute | solution.py:113
  28.0 1.7 %collective-permute-start.3 = (bf16[18,5,256]{2,1,0:T(8,128)(2,1)S(1)}, bf16[18,5,256]{2,1,0:T(8,128)(2,1)S(1)}, u32[]{:S(2)}, u32[]{:S(2)}) collective-permute-start(bf16[18,5,256]{2,1,0:T(8,128)(2,1)S(1)} %get-tuple-element.30), channel_id=1, source_target_pairs={{4,0},{8,4},{12,8},{0,12},{5,1},{9,5},{13,9},{1,13},{6,2},{10,6},{... | collective-permute-start | bytes 138248 | tf_op jit(solution)/shard_map/ppermute | solution.py:114
  29.8 1.4 %collective-permute-done.2 = bf16[18,5,256]{2,1,0:T(8,128)(2,1)S(1)} collective-permute-done((bf16[18,5,256]{2,1,0:T(8,128)(2,1)S(1)}, bf16[18,5,256]{2,1,0:T(8,128)(2,1)S(1)}, u32[]{:S(2)}, u32[]{:S(2)}) %collective-permute-start.2) | collective-permute-done | bytes 46112 | tf_op jit(solution)/shard_map/ppermute | solution.py:113
  32.4 6.6 %divide_multiply_fusion = (f32[4,16,24,512]{3,0,2,1:T(4,128)S(1)}, f32[4,16,24,512]{3,0,2,1:T(4,128)}) fusion(bf16[3,3,72,512]{3,2,1,0:T(8,128)(2,1)S(1)} %bitcast.279, bf16[1,18,26,72]{3,0,2,1:T(2,128)(2,1)S(1)} %copy.703, bf16[1,18,26,72]{3,0,2,1:T(2,128)(2,1)S(1)} %copy.702, bf16[1,18,26,72]{3,0,2,1:T(2,128)(2,1)S(1)} %copy.701, ...), kind=kOutput, calls=%fused_computation | convolution fusion | flops 1023439872 | bytes 7224576 | tf_op jit(solution)/shard_map/conv_general_dilated | solution.py:163
  39.0 0.4 slice_add_fusion
  39.5 0.5 reduce_sum.91
  41.5 1.5 %stack.121 = bf16[8,8,12,192]{3,0,2,1:T(8,128)(2,1)S(1)} concatenate(bf16[1,8,12,192]{3,0,2,1:T(2,128)(2,1)S(1)} %copy.710, bf16[1,8,12,192]{3,0,2,1:T(2,128)(2,1)S(1)} %copy.711, bf16[1,8,12,192]{3,0,2,1:T(2,128)(2,1)S(1)} %copy.712, bf16[1,8,12,192]{3,0,2,1:T(2,128)(2,1)S(1)} %copy.713, bf16[1,8,12,192]{3,0,2,1:T(2,128)(2,1)S(1)} %copy.714, bf16[1,8,12,192]{3,0,2,1:T(2,128)(2,1)S(1)} %copy.715, ...), dimensions={0} | concatenate | bytes 589824 | tf_op jit(solution)/shard_map/stack | solution.py:199
  43.0 1.5 %multiply_convert_fusion = (bf16[8,6,10,256]{3,0,2,1:T(8,128)(2,1)S(1)}, f32[8,6,10,256]{3,0,2,1:T(8,128)}) fusion(bf16[8,8,12,128]{3,0,2,1:T(8,128)(2,1)S(1)} %bitcast.257, bf16[8,8,12,192]{3,0,2,1:T(8,128)(2,1)S(1)} %stack.121, bf16[3,3,192,256]{3,2,1,0:T(8,128)(2,1)S(1)} %bitcast.277), kind=kOutput, calls=%fused_computation.20 | convolution fusion | flops 426393600 | bytes 2113536 | tf_op jit(solution)/shard_map/conv_general_dilated | solution.py:163
  44.6 0.6 fusion.11
  45.2 0.5 fusion.42
  46.1 0.4 select_reduce_fusion.2
  46.6 0.4 copy-done.8
  47.0 0.9 fusion.43
  49.6 3.5 %fusion.3 = f32[3,3,72,512]{3,2,1,0:T(8,128)S(1)} fusion(f32[4,8,16,256]{3,0,2,1:T(4,128)S(1)} %bitcast.251, f32[4,16,24,512]{3,0,2,1:T(4,128)} %get-tuple-element.68, bf16[1,18,26,72]{3,0,2,1:T(2,128)(2,1)S(1)} %copy-done.5, bf16[1,18,26,72]{3,0,2,1:T(2,128)(2,1)S(1)} %copy-done.3, bf16[1,18,26,72]{3,0,2,1:T(2,128)(2,1)S(1)} %copy.701, ...), kind=kOutput, calls=%fused_computation.19 | convolution fusion | flops 343700480 | bytes 3169536 | tf_op jit(solution)/shard_map/conv_general_dilated | solution.py:174
  54.0 0.9 select_reduce_fusion.5
  55.4 0.7 pad_maximum_fusion.3
  56.2 30.3 %sum_over_devices.1 = f32[16,32,128]{2,1,0:T(8,128)} custom-call(f32[16,32,128]{2,1,0:T(8,128)} %bitcast.247), custom_call_target="tpu_custom_call" | custom-call | tf_op jit(solution)/shard_map/sum_over_devices/pallas_call | solution.py:84
  86.5 1.7 %slice.175 = f32[32,2048]{1,0:T(8,128)} reshape(f32[16,32,128]{2,1,0:T(8,128)} %sum_over_devices.1) | data formatting | bytes 524288 | tf_op jit(solution)/shard_map/slice | solution.py:102
  88.2 1.3 %slice.200 = f32[27,128]{1,0:T(8,128)} slice(f32[512,128]{1,0:T(8,128)} %bitcast.245), slice={[432:459], [0:128]} | slice | bytes 27648 | tf_op jit(solution)/shard_map/slice | solution.py:101
  89.8 0.6 copy-done.16
  (140 shorter events, 7.1 us)
Async XLA Ops:
  1.5 25.2 %collective-permute-start = (bf16[5,16,256]{2,1,0:T(8,128)(2,1)S(1)}, bf16[5,16,256]{2,1,0:T(8,128)(2,1)S(1)}, u32[]{:S(2)}, u32[]{:S(2)}) collective-permute-start(bf16[5,16,256]{2,1,0:T(8,128)(2,1)S(1)} %get-tuple-element.49), channel_id=1, source_target_pairs={{0,16},{16,32},{32,48},{48,64},{64,80},{80,96},{96,112},{112,128},... | collective-permute-start | bytes 122888 | tf_op jit(solution)/shard_map/ppermute | solution.py:113
  3.6 23.1 %collective-permute-start.1 = (bf16[5,16,256]{2,1,0:T(8,128)(2,1)S(1)}, bf16[5,16,256]{2,1,0:T(8,128)(2,1)S(1)}, u32[]{:S(2)}, u32[]{:S(2)}) collective-permute-start(bf16[5,16,256]{2,1,0:T(8,128)(2,1)S(1)} %get-tuple-element.50), channel_id=1, source_target_pairs={{16,0},{32,16},{48,32},{64,48},{80,64},{96,80},{112,96},{128,112},... | collective-permute-start | bytes 122888 | tf_op jit(solution)/shard_map/ppermute | solution.py:114
  11.6 10.9 %collective-permute-start.4 = (bf16[1,4,1024]{2,1,0:T(4,128)(2,1)S(1)}, bf16[1,4,1024]{2,1,0:T(4,128)(2,1)S(1)}, u32[]{:S(2)}, u32[]{:S(2)}) collective-permute-start(bf16[1,4,1024]{2,1,0:T(4,128)(2,1)S(1)} %get-tuple-element.57), channel_id=1, source_target_pairs={{0,16},{16,32},{32,48},{48,64},{64,80},{80,96},{96,112},{112,128},... | collective-permute-start | bytes 24584 | tf_op jit(solution)/shard_map/ppermute | solution.py:113
  11.7 10.8 %collective-permute-start.5 = (bf16[1,4,1024]{2,1,0:T(4,128)(2,1)S(1)}, bf16[1,4,1024]{2,1,0:T(4,128)(2,1)S(1)}, u32[]{:S(2)}, u32[]{:S(2)}) collective-permute-start(bf16[1,4,1024]{2,1,0:T(4,128)(2,1)S(1)} %get-tuple-element.58), channel_id=1, source_target_pairs={{16,0},{32,16},{48,32},{64,48},{80,64},{96,80},{112,96},{128,112},... | collective-permute-start | bytes 24584 | tf_op jit(solution)/shard_map/ppermute | solution.py:114
  20.3 2.0 %copy-start.15 = (bf16[32,512,1,1]{1,0,3,2:T(8,128)(2,1)S(1)}, bf16[32,512,1,1]{1,0,3,2:T(8,128)(2,1)}, u32[]{:S(2)}) copy-start(bf16[32,512,1,1]{1,0,3,2:T(8,128)(2,1)} %constant.84) | copy-start | bytes 98308
  20.3 2.2 %copy-start.6 = (bf16[1,2,4,1024]{3,2,1,0:T(4,128)(2,1)S(1)}, bf16[1,2,4,1024]{3,2,1,0:T(4,128)(2,1)}, u32[]{:S(2)}) copy-start(bf16[1,2,4,1024]{3,2,1,0:T(4,128)(2,1)} %param.21) | copy-start | bytes 49156
  20.3 5.1 %copy-start.17 = (pred[3,72,512]{2,1,0:T(8,128)(4,1)S(1)}, pred[3,72,512]{2,1,0:T(8,128)(4,1)}, u32[]{:S(2)}) copy-start(pred[3,72,512]{2,1,0:T(8,128)(4,1)} %constant.76) | copy-start | bytes 331780
  20.3 5.1 %copy-start.18 = (bf16[72,4,1,1]{0,1,3,2:T(4,128)(2,1)S(1)}, bf16[72,4,1,1]{0,1,3,2:T(4,128)(2,1)}, u32[]{:S(2)}) copy-start(bf16[72,4,1,1]{0,1,3,2:T(4,128)(2,1)} %constant.85) | copy-start | bytes 1732
  22.5 3.7 %copy-start.11 = (pred[6,32,256]{2,1,0:T(32,128)(4,1)S(1)}, pred[6,32,256]{2,1,0:T(32,128)(4,1)}, u32[]{:S(2)}) copy-start(pred[6,32,256]{2,1,0:T(32,128)(4,1)} %constant.78) | copy-start | bytes 147460
  22.5 3.7 %copy-start.10 = (pred[6,32,256]{2,1,0:T(32,128)(4,1)S(1)}, pred[6,32,256]{2,1,0:T(32,128)(4,1)}, u32[]{:S(2)}) copy-start(pred[6,32,256]{2,1,0:T(32,128)(4,1)} %constant.80) | copy-start | bytes 147460
  22.6 3.7 %copy-start.9 = (pred[6,32,256]{2,1,0:T(32,128)(4,1)S(1)}, pred[6,32,256]{2,1,0:T(32,128)(4,1)}, u32[]{:S(2)}) copy-start(pred[6,32,256]{2,1,0:T(32,128)(4,1)} %constant.79) | copy-start | bytes 147460
  22.6 3.9 %collective-permute-start.6 = (bf16[4,1,1024]{2,1,0:T(2,128)(2,1)S(1)}, bf16[4,1,1024]{2,1,0:T(2,128)(2,1)S(1)}, u32[]{:S(2)}, u32[]{:S(2)}) collective-permute-start(bf16[4,1,1024]{2,1,0:T(2,128)(2,1)S(1)} %get-tuple-element.55), channel_id=1, source_target_pairs={{0,4},{4,8},{8,12},{12,0},{1,5},{5,9},{9,13},{13,1},{2,6},{6,10},{... | collective-permute-start | bytes 24584 | tf_op jit(solution)/shard_map/ppermute | solution.py:113
  23.9 2.8 %copy-start = (bf16[1,8,16,256]{3,2,1,0:T(8,128)(2,1)S(1)}, bf16[1,8,16,256]{3,2,1,0:T(8,128)(2,1)}, u32[]{:S(2)}) copy-start(bf16[1,8,16,256]{3,2,1,0:T(8,128)(2,1)} %param.18) | copy-start | bytes 196612
  23.9 2.6 %collective-permute-start.7 = (bf16[4,1,1024]{2,1,0:T(2,128)(2,1)S(1)}, bf16[4,1,1024]{2,1,0:T(2,128)(2,1)S(1)}, u32[]{:S(2)}, u32[]{:S(2)}) collective-permute-start(bf16[4,1,1024]{2,1,0:T(2,128)(2,1)S(1)} %get-tuple-element.56), channel_id=1, source_target_pairs={{4,0},{8,4},{12,8},{0,12},{5,1},{9,5},{13,9},{1,13},{6,2},{10,6},{... | collective-permute-start | bytes 24584 | tf_op jit(solution)/shard_map/ppermute | solution.py:114
  26.8 4.5 %collective-permute-start.2 = (bf16[18,5,256]{2,1,0:T(8,128)(2,1)S(1)}, bf16[18,5,256]{2,1,0:T(8,128)(2,1)S(1)}, u32[]{:S(2)}, u32[]{:S(2)}) collective-permute-start(bf16[18,5,256]{2,1,0:T(8,128)(2,1)S(1)} %get-tuple-element.29), channel_id=1, source_target_pairs={{0,4},{4,8},{8,12},{12,0},{1,5},{5,9},{9,13},{13,1},{2,6},{6,10},{... | collective-permute-start | bytes 138248 | tf_op jit(solution)/shard_map/ppermute | solution.py:113
  28.0 3.2 %collective-permute-start.3 = (bf16[18,5,256]{2,1,0:T(8,128)(2,1)S(1)}, bf16[18,5,256]{2,1,0:T(8,128)(2,1)S(1)}, u32[]{:S(2)}, u32[]{:S(2)}) collective-permute-start(bf16[18,5,256]{2,1,0:T(8,128)(2,1)S(1)} %get-tuple-element.30), channel_id=1, source_target_pairs={{4,0},{8,4},{12,8},{0,12},{5,1},{9,5},{13,9},{1,13},{6,2},{10,6},{... | collective-permute-start | bytes 138248 | tf_op jit(solution)/shard_map/ppermute | solution.py:114
  32.2 6.8 %copy-start.2 = (bf16[1,18,26,72]{3,0,2,1:T(2,128)(2,1)}, bf16[1,18,26,72]{3,0,2,1:T(2,128)(2,1)S(1)}, u32[]{:S(2)}) copy-start(bf16[1,18,26,72]{3,0,2,1:T(2,128)(2,1)S(1)} %copy.702) | copy-start | bytes 202180
  32.4 6.6 %copy-start.4 = (bf16[1,18,26,72]{3,0,2,1:T(2,128)(2,1)}, bf16[1,18,26,72]{3,0,2,1:T(2,128)(2,1)S(1)}, u32[]{:S(2)}) copy-start(bf16[1,18,26,72]{3,0,2,1:T(2,128)(2,1)S(1)} %copy.703) | copy-start | bytes 202180
  46.1 0.9 %copy-start.8 = (f32[256,64]{1,0:T(8,128)S(1)}, f32[256,64]{1,0:T(8,128)}, u32[]{:S(2)}) copy-start(f32[256,64]{1,0:T(8,128)} %constant.57.clone) | copy-start | bytes 196612
  48.6 1.0 %copy-start.3 = (bf16[1,18,26,72]{3,0,2,1:T(2,128)(2,1)S(1)}, bf16[1,18,26,72]{3,0,2,1:T(2,128)(2,1)}, u32[]{:S(2)}) copy-start(bf16[1,18,26,72]{3,0,2,1:T(2,128)(2,1)} %copy-done.2) | copy-start | bytes 202180
  48.6 1.1 %copy-start.5 = (bf16[1,18,26,72]{3,0,2,1:T(2,128)(2,1)S(1)}, bf16[1,18,26,72]{3,0,2,1:T(2,128)(2,1)}, u32[]{:S(2)}) copy-start(bf16[1,18,26,72]{3,0,2,1:T(2,128)(2,1)} %copy-done.4) | copy-start | bytes 202180
  53.2 0.8 copy-start.12
  53.2 0.8 copy-start.13
  53.2 0.8 copy-start.14
  54.0 1.0 %copy-start.1 = (f32[512,32]{1,0:T(8,128)S(1)}, f32[512,32]{1,0:T(8,128)}, u32[]{:S(2)}) copy-start(f32[512,32]{1,0:T(8,128)} %constant.61.clone) | copy-start | bytes 196612
  54.8 34.7 %copy-start.7 = (f32[8,6,10,256]{3,0,2,1:T(8,128)S(1)}, f32[8,6,10,256]{3,0,2,1:T(8,128)}, u32[]{:S(2)}) copy-start(f32[8,6,10,256]{3,0,2,1:T(8,128)} %get-tuple-element.70) | copy-start | bytes 1474564
  89.8 0.6 copy-start.16
where the time goes:
time: 90.9 us; the launch traced here: 90.4 us
  Pallas kernels  30.3 us (33%)
  starting transfers between devices  20.9 us (23%)
  matrix products  16.9 us (19%)
  local copies, waits for them, and re-layouts  15.3 us (17%)
  other arithmetic  3.86 us (4%)
  waiting for transfers between devices  1.68 us (2%)
  between operations  1.53 us (2%)
    pallas_call x1, Pallas kernels, sum_over_devices(): pl.pallas_call(sum_kernel, out_shape=jax.ShapeDtypeStruct(block, jnp.floa...  30.3 us
    ppermute x4, starting transfers between devices, padded_2(): after = lax.ppermute(first, axis, down)  16.1 us
    conv_general_dilated x3, matrix products, convolve(): lax.conv_general_dilated(padded, weight, (1, 1), padding, dimension_numbe...  8.64 us
    ppermute x4, starting transfers between devices, padded_2(): before = lax.ppermute(last, axis, up)  4.77 us
    conv_general_dilated x2, matrix products, weight_gradient(): lax.conv_general_dilated(padded, grad, (1, 1), 'VALID', dimension_numbers...  4.1 us
    unnamed x78, local copies, waits for them, and re-layouts  3.72 us
    another operation x15, local copies, waits for them, and re-layouts, chunks(): jnp.stack([values[..., j * step:j * step + width] for j in range(count)])  3.05 us
    dot_general x2, matrix products, banded(): jnp.einsum('ri,kcin->kcrn', spread_rows, wide, preferred_element_type=jnp...  2.72 us
  transfers between devices with their start and end apart: 8, of which 2 were waited for; matrix products, arithmetic and copies ran while one was open for 8% of the time, Pallas kernels for 0%

commit v1 on v0

--- a/solution.py
+++ b/solution.py
@@ -14,7 +14,7 @@
 CHUNK = 32
 
 
-def sum_kernel(x_ref, out_ref, near, part, far, gathered, sends, recvs):
+def sum_kernel(first, second, first_out, second_out, x_ref, near, part, far, gathered, sends, recvs):
     row = lax.axis_index("gx")
     column = lax.axis_index("gy")
     sample = lax.axis_index("sa")
@@ -32,6 +32,12 @@
     for k in range(1, 16):
         pl.semaphore_signal(barrier, inc=1, device_id=plane_peer(k)[1], device_id_type=MESH)
         pl.semaphore_signal(barrier, inc=1, device_id=row_peer(k)[1], device_id_type=MESH)
+    x_ref[...] = jnp.zeros_like(x_ref)
+    for g in range(16):
+        x_ref[g, 0:27] = second[:, 128 * g : 128 * g + 128]
+        rows = min(2, 27 - 2 * g)
+        if rows > 0:
+            x_ref[g, 27 : 27 + rows] = first[2 * g : 2 * g + rows]
     pl.semaphore_wait(barrier, 30)
 
     def send(stage, k, source, target, device):
@@ -72,21 +78,28 @@
         third.append(send(2, k, gathered.at[me], gathered.at[me], device))
     for copy in third:
         copy.wait_recv()
-    out_ref[...] = gathered[...]
+    for g in range(16):
+        second_out[:, 128 * g : 128 * g + 128] = gathered[g, 0:27]
+        rows = min(2, 27 - 2 * g)
+        if rows > 0:
+            first_out[2 * g : 2 * g + rows] = gathered[g, 27 : 27 + rows]
     for copy in copies + second + third:
         copy.wait_send()
 
 
 def sum_over_devices(first, second):
-    filler = jnp.zeros((16 * CHUNK * 128 - first.size - second.size,), jnp.float32)
-    flat = jnp.concatenate([second.reshape(-1), first.reshape(-1), filler])
     block = (16, CHUNK, 128)
-    total = pl.pallas_call(
+    whole = pl.BlockSpec(memory_space=pltpu.VMEM)
+    return pl.pallas_call(
         sum_kernel,
-        out_shape=jax.ShapeDtypeStruct(block, jnp.float32),
-        in_specs=[pl.BlockSpec(memory_space=pltpu.VMEM)],
-        out_specs=pl.BlockSpec(memory_space=pltpu.VMEM),
+        out_shape=(
+            jax.ShapeDtypeStruct(first.shape, jnp.float32),
+            jax.ShapeDtypeStruct(second.shape, jnp.float32),
+        ),
+        in_specs=[whole, whole],
+        out_specs=(whole, whole),
         scratch_shapes=[
+            pltpu.VMEM(block, jnp.float32),
             pltpu.VMEM(block, jnp.float32),
             pltpu.VMEM(block[1:], jnp.float32),
             pltpu.VMEM(block, jnp.float32),
@@ -96,24 +109,89 @@
         ],
         compiler_params=pltpu.CompilerParams(collective_id=0, has_side_effects=True),
         name="sum_over_devices",
-    )(flat.reshape(block)).reshape(-1)
-    return (
-        total[second.size : second.size + first.size].reshape(first.shape),
-        total[: second.size].reshape(second.shape),
+    )(first, second)
+
+
+def halo_kernel(volume, low, high, outer, outer_low, outer_high, *refs):
+    outs, slots, sends, recvs = refs[:8], refs[8:16], refs[16], refs[17]
+    row = lax.axis_index("gx")
+    column = lax.axis_index("gy")
+    sample = lax.axis_index("sa")
+    rows = lax.axis_size("gx")
+    columns = lax.axis_size("gy")
+
+    def device(dx, dy):
+        return ((row + rows + dx) % rows, (column + columns + dy) % columns, sample)
+
+    barrier = pltpu.get_barrier_semaphore()
+    around = [(dx, dy) for dx in (-1, 0, 1) for dy in (-1, 0, 1) if (dx, dy) != (0, 0)]
+    for dx, dy in around:
+        pl.semaphore_signal(barrier, inc=1, device_id=device(dx, dy), device_id_type=MESH)
+    pl.semaphore_wait(barrier, 8)
+    copies = []
+
+    def send(source, target, dx, dy):
+        k = len(copies)
+        copy = pltpu.make_async_remote_copy(
+            src_ref=source,
+            dst_ref=target,
+            send_sem=sends.at[k],
+            recv_sem=recvs.at[k],
+            device_id=device(dx, dy),
+            device_id_type=MESH,
+        )
+        copy.start()
+        copies.append(copy)
+
+    groups = (
+        (volume, low, high, slots[:4]),
+        (outer, outer_low, outer_high, slots[4:]),
     )
-
-
-def padded_2(x, sides, width):
-    for axis, dim in sides:
-        peers, length = (lax.axis_size(axis), x.shape[dim])
-        up = [(i, (i + 1) % peers) for i in range(peers)]
-        down = [(j, i) for i, j in up]
-        last = lax.slice_in_dim(x, length - width, length, axis=dim)
-        first = lax.slice_in_dim(x, 0, width, axis=dim)
-        before = lax.ppermute(last, axis, up)
-        after = lax.ppermute(first, axis, down)
-        x = jnp.concatenate([before, x, after], axis=dim)
-    return x
+    for whole, first, last, (left, right, top, bottom) in groups:
+        size = whole.shape[0]
+        width = top.shape[0]
+        tail = pl.ds(size - width, width)
+        head = pl.ds(0, width)
+        end = pl.ds(size + width, width)
+        send(whole.at[tail], top, 1, 0)
+        send(whole.at[head], bottom, -1, 0)
+        send(last, left.at[pl.ds(width, size)], 0, 1)
+        send(first, right.at[pl.ds(width, size)], 0, -1)
+        send(last.at[tail], left.at[head], 1, 1)
+        send(last.at[head], left.at[end], -1, 1)
+        send(first.at[tail], right.at[head], 1, -1)
+        send(first.at[head], right.at[end], -1, -1)
+    for copy in copies:
+        copy.wait_recv()
+    for out, slot in zip(outs, slots):
+        out[...] = slot[...]
+    for copy in copies:
+        copy.wait_send()
+
+
+def exchange(volume, outer):
+    args = []
+    shapes = []
+    for x, width in ((volume, 5), (outer, 1)):
+        rows, columns, lanes = x.shape
+        args += [x, x[:, :width], x[:, columns - width :]]
+        shapes += [(rows + 2 * width, width, lanes)] * 2 + [(width, columns, lanes)] * 2
+    space = pl.BlockSpec(memory_space=pltpu.VMEM)
+    pieces = pl.pallas_call(
+        halo_kernel,
+        out_shape=tuple(jax.ShapeDtypeStruct(shape, jnp.bfloat16) for shape in shapes),
+        in_specs=[space] * 6,
+        out_specs=(space,) * 8,
+        scratch_shapes=[pltpu.VMEM(shape, jnp.bfloat16) for shape in shapes]
+        + [pltpu.SemaphoreType.DMA((16,)), pltpu.SemaphoreType.DMA((16,))],
+        compiler_params=pltpu.CompilerParams(collective_id=1, has_side_effects=True),
+        name="exchange",
+    )(*args)
+    result = []
+    for x, (left, right, top, bottom) in ((volume, pieces[:4]), (outer, pieces[4:])):
+        middle = jnp.concatenate([top, x, bottom], axis=0)
+        result.append(jnp.concatenate([left, middle, right], axis=1))
+    return result
 
 
 PLANES_ONE = 16
@@ -209,11 +287,9 @@
 
 
 def body(volume, first_kernel, second_kernel, cotangent):
-    sides = (("gx", 0), ("gy", 1))
     weight_one = banded(first_kernel, PLANES_ONE, CH_IN, CH_ONE)
     weight_two = banded(second_kernel, PLANES_TWO, CH_ONE, CH_TWO)
-    outer = padded_2(cotangent[0], sides, 1)
-    fields = padded_2(volume[0], sides, 5)
+    fields, outer = exchange(volume[0], cotangent[0])
     count = fields.shape[-1] // (PLANES_ONE * CH_IN)
     fields = chunks(fields, (PLANES_ONE + 2) * CH_IN, CH_IN, count)
     first_pre = convolve(fields, weight_one)

time: 90.9 us -> 80.1 us (0.88)
  starting transfers between devices: 20.9 us -> 0 us
  Pallas kernels: 30.3 us -> 45.7 us
  matrix products: 16.9 us -> 14.5 us
  local copies, waits for them, and re-layouts: 15.3 us -> 13.6 us
  waiting for transfers between devices: 1.68 us -> 0 us
    ppermute x8 -> x0, starting transfers between devices: 20.9 us -> none  [the longest x4 16.1 us: padded_2(): after = lax.ppermute(first, axis, down)]
    pallas_call x1 -> x2, Pallas kernels: 30.3 us -> 45.7 us  [the longest x1 28.3 us: sum_over_devices(): pl.pallas_call(sum_kernel, out_shape=(jax.ShapeDtypeStruct(first.shape, j...]
    slice x6 -> x2, local copies, waits for them, and re-layouts: 4.65 us -> 2.82 us  [exchange(): args += [x, x[:, :width], x[:, columns - width:]]]
    ppermute x8 -> x0, waiting for transfers between devices: 1.68 us -> none  [the longest x4 1.67 us: padded_2(): before = lax.ppermute(last, axis, up)]
    dot_general x2, local copies, waits for them, and re-layouts: 1.94 us -> 0.29 us  [banded(): jnp.dot(kernel.reshape(27 * inputs, outputs), jnp.asarray(spread_columns,...]
    reshape x0 -> x2, local copies, waits for them, and re-layouts: none -> 1.55 us  [unbanded(): return narrow.reshape(27, inputs * outputs)]
    unnamed x78 -> x88, local copies, waits for them, and re-layouts: 3.72 us -> 4.96 us
    conv_general_dilated x3, matrix products: 8.64 us -> 7.64 us  [convolve(): lax.conv_general_dilated(padded, weight, (1, 1), padding, dimension_numbe...]
  transfers between devices with their start and end apart: 8 -> 0, of which waited for: 2 -> 0; matrix products, arithmetic and copies ran while one was open for 8% -> 0% of each run, Pallas kernels for 0% -> 0%
where the time goes in v1:
time: 80.1 us; the launch traced here: 79.5 us
  Pallas kernels  45.7 us (57%)
  matrix products  14.5 us (18%)
  local copies, waits for them, and re-layouts  13.6 us (17%)
  other arithmetic  4.23 us (5%)
  between operations  1.51 us (2%)
    pallas_call x1, Pallas kernels, sum_over_devices(): pl.pallas_call(sum_kernel, out_shape=(jax.ShapeDtypeStruct(first.shape, j...  28.3 us
    pallas_call x1, Pallas kernels, exchange(): pl.pallas_call(halo_kernel, out_shape=tuple((jax.ShapeDtypeStruct(shape,...  17.4 us
    conv_general_dilated x3, matrix products, convolve(): lax.conv_general_dilated(padded, weight, (1, 1), padding, dimension_numbe...  7.64 us
    unnamed x88, local copies, waits for them, and re-layouts  4.96 us
    conv_general_dilated x2, matrix products, weight_gradient(): lax.conv_general_dilated(padded, grad, (1, 1), 'VALID', dimension_numbers...  3.59 us
    slice x2, local copies, waits for them, and re-layouts, exchange(): args += [x, x[:, :width], x[:, columns - width:]]  2.82 us
    another operation x11, local copies, waits for them, and re-layouts, chunks(): jnp.stack([values[..., j * step:j * step + width] for j in range(count)])  2.27 us
    dot_general x2, matrix products, banded(): jnp.einsum('ri,kcin->kcrn', spread_rows, wide, preferred_element_type=jnp...  1.84 us

profile of v1, /device:TPU:1, one launch (start us, length us, event | category | flops | bytes accessed | tf_op | source)
XLA Modules:
  0.0 79.5 jit_solution(4696746878747748010)
XLA Ops:
  0.7 1.4 %fusion.41 = (bf16[8,5,256]{2,1,0:T(8,128)(2,1)}, bf16[8,5,256]{2,1,0:T(8,128)(2,1)}) fusion(bf16[8,16,256]{2,1,0:T(8,128)(2,1)} %bitcast.235), kind=kLoop, calls=%fused_computation.157 | loop fusion | bytes 81920 | tf_op jit(solution)/shard_map/slice | solution.py:177
  2.1 1.4 %fusion.43 = (bf16[2,1,1024]{2,1,0:T(2,128)(2,1)}, bf16[2,1,1024]{2,1,0:T(2,128)(2,1)}) fusion(bf16[2,4,1024]{2,1,0:T(4,128)(2,1)} %bitcast.245), kind=kLoop, calls=%fused_computation.159 | loop fusion | bytes 16384 | tf_op jit(solution)/shard_map/slice | solution.py:177
  3.5 17.4 %exchange.1 = (bf16[18,5,256]{2,1,0:T(8,128)(2,1)}, bf16[18,5,256]{2,1,0:T(8,128)(2,1)}, bf16[5,16,256]{2,1,0:T(8,128)(2,1)}, bf16[5,16,256]{2,1,0:T(8,128)(2,1)...) custom-call(bf16[8,16,256]{2,1,0:T(8,128)(2,1)} %bitcast.236, ...), custom_call_target="tpu_custom_call" | custom-call | tf_op jit(solution)/shard_map/exchange/pallas_call | solution.py:180
  20.9 1.1 %pad_maximum_fusion.2 = bf16[18,26,256]{2,1,0:T(8,128)(2,1)S(1)} fusion(bf16[18,5,256]{2,1,0:T(8,128)(2,1)} %get-tuple-element.16, bf16[5,16,256]{2,1,0:T(8,128)(2,1)} %get-tuple-element.15, bf16[8,16,256]{2,1,0:T(8,128)(2,1)} %bitcast.237, bf16[5,16,256]{2,1,0:T(8,128)(2,1)} %get-tuple-element.14, bf16[18,5,256]{2,1,0:T(8,128)(2,1)} %get-tuple-element.13), kind=kLoop, calls=%fused_computation.29 | loop fusion | flops 1198080 | bytes 479232 | tf_op jit(solution)/shard_map/concatenate | solution.py:193
  22.0 0.2 fusion.12
  22.7 0.8 fusion.1
  23.5 5.6 %divide_multiply_fusion = (f32[4,16,24,512]{3,0,2,1:T(4,128)S(1)}, f32[4,16,24,512]{3,0,2,1:T(4,128)}) fusion(bf16[3,3,72,512]{3,2,1,0:T(8,128)(2,1)S(1)} %bitcast.267, bf16[4,18,26,72]{3,2,1,0:T(8,128)(2,1)S(1)} %pad_maximum_fusion.1), kind=kOutput, calls=%fused_computation | convolution fusion | flops 1022361600 | bytes 7224576 | tf_op jit(solution)/shard_map/conv_general_dilated | solution.py:241
  29.1 0.4 slice_add_fusion
  29.6 0.4 reduce_sum.91
  30.2 0.3 fusion.40
  30.6 0.2 fusion.23
  31.7 1.4 %stack.121 = bf16[8,8,12,192]{3,0,2,1:T(8,128)(2,1)S(1)} concatenate(bf16[1,8,12,192]{3,0,2,1:T(2,128)(2,1)S(1)} %copy.679, bf16[1,8,12,192]{3,0,2,1:T(2,128)(2,1)S(1)} %copy.680, bf16[1,8,12,192]{3,0,2,1:T(2,128)(2,1)S(1)} %copy.681, bf16[1,8,12,192]{3,0,2,1:T(2,128)(2,1)S(1)} %copy.682, bf16[1,8,12,192]{3,0,2,1:T(2,128)(2,1)S(1)} %copy.683, bf16[1,8,12,192]{3,0,2,1:T(2,128)(2,1)S(1)} %copy.684, ...), dimensions={0} | concatenate | bytes 589824 | tf_op jit(solution)/shard_map/stack | solution.py:277
  33.5 0.2 dot_general.25
  33.8 1.1 %fusion = bf16[9,192,256]{2,1,0:T(8,128)(2,1)S(1)} fusion(pred[3,192,256]{2,1,0:T(8,128)(4,1)S(1)} %copy.797, bf16[192,32,1,1]{0,1,3,2:T(8,128)(2,1)S(1)} %copy-done.21, bf16[64,256,1,1]{1,0,3,2:T(8,128)(2,1)S(1)} %copy-done.20, bf16[9,3,32,64]{3,2,1,0:T(8,128)(2,1)S(1)} %dot_general.25), kind=kOutput, calls=%fused_computation.2 | convolution fusion | flops 115458048 | bytes 1187840 | tf_op jit(solution)/shard_map/ri,kcin->kcrn/dot_general | solution.py:220
  34.8 1.5 %multiply_convert_fusion = (bf16[8,6,10,256]{3,0,2,1:T(8,128)(2,1)S(1)}, f32[8,6,10,256]{3,0,2,1:T(8,128)}) fusion(bf16[8,8,12,128]{3,0,2,1:T(8,128)(2,1)S(1)} %bitcast.244, bf16[8,8,12,192]{3,0,2,1:T(8,128)(2,1)S(1)} %stack.121, bf16[3,3,192,256]{3,2,1,0:T(8,128)(2,1)S(1)} %bitcast.265), kind=kOutput, calls=%fused_computation.21 | convolution fusion | flops 426393600 | bytes 2113536 | tf_op jit(solution)/shard_map/conv_general_dilated | solution.py:241
  36.4 0.6 fusion.14
  36.9 0.2 copy-done.8
  37.3 0.4 select_reduce_fusion.2
  37.7 0.4 copy-done.4
  38.2 0.9 %fusion.46 = f32[864,64]{1,0:T(8,128)S(1)} fusion(f32[864,256]{1,0:T(8,128)S(1)} %bitcast.229, f32[256,64]{1,0:T(8,128)S(1)} %copy-done.4), kind=kOutput, calls=%fused_computation.162 | convolution fusion | flops 169869312 | bytes 1171456 | tf_op jit(solution)/shard_map/dot_general | solution.py:231
  39.0 0.9 %reshape.69.second = f32[27,2048]{1,0:T(8,128)} reshape(f32[864,64]{1,0:T(8,128)S(1)} %fusion.46) | data formatting | bytes 442368 | tf_op jit(solution)/shard_map/reshape | solution.py:237
  39.9 0.5 fusion.44
  41.0 0.3 fusion.39
  42.0 3.0 %fusion.3 = f32[3,3,72,512]{3,2,1,0:T(8,128)S(1)} fusion(f32[4,8,16,256]{3,0,2,1:T(4,128)S(1)} %bitcast.239, f32[4,16,24,512]{3,0,2,1:T(4,128)} %get-tuple-element.84, bf16[4,18,26,72]{3,2,1,0:T(8,128)(2,1)S(1)} %pad_maximum_fusion.1), kind=kOutput, calls=%fused_computation.20 | convolution fusion | flops 342622208 | bytes 3169536 | tf_op jit(solution)/shard_map/conv_general_dilated | solution.py:252
  45.0 0.4 reshape.64
  45.4 0.3 copy-done.9
  45.8 0.9 %select_reduce_fusion.5 = (f32[9,4,512]{2,1,0:T(4,128)S(1)}, f32[9,4,512]{2,1,0:T(4,128)S(1)}, f32[9,4,512]{2,1,0:T(4,128)S(1)}) fusion(f32[9,18,4,512]{3,2,1,0:T(4,128)S(1)} %reshape.64, pred[18,4,512]{2,1,0:T(4,128)(4,1)S(1)} %copy-done.9, pred[18,4,512]{2,1,0:T(4,128)(4,1)S(1)} %copy-done.11, pred[18,4,512]{2,1,0:T(4,128)(4,1)S(1)} %copy-done.10), kind=kLoop, calls=%fused_computation.11 | loop fusion | flops 1935360 | bytes 1658880 | tf_op jit(solution)/shard_map/reduce_sum | solution.py:229
  46.8 0.4 fusion.45
  47.2 0.7 reshape.66.first
  47.9 28.3 %sum_over_devices.1 = (f32[27,128]{1,0:T(8,128)}, f32[27,2048]{1,0:T(8,128)}) custom-call(f32[27,128]{1,0:T(8,128)} %reshape.66.first, f32[27,2048]{1,0:T(8,128)} %reshape.69.second), custom_call_target="tpu_custom_call" | custom-call | tf_op jit(solution)/shard_map/sum_over_devices/pallas_call | solution.py:93
  76.5 1.3 %copy.801 = f32[27,128]{1,0:T(8,128)} copy(f32[27,128]{1,0:T(8,128)} %get-tuple-element.95) | data formatting | bytes 27648
  77.9 1.7 %copy.802 = f32[27,2048]{1,0:T(8,128)} copy(f32[27,2048]{1,0:T(8,128)} %get-tuple-element.96) | data formatting | bytes 442368
  (124 shorter events, 3.3 us)
Async XLA Ops:
  0.6 21.9 %copy-start.12 = (bf16[32,512,1,1]{1,0,3,2:T(8,128)(2,1)S(1)}, bf16[32,512,1,1]{1,0,3,2:T(8,128)(2,1)}, u32[]{:S(2)}) copy-start(bf16[32,512,1,1]{1,0,3,2:T(8,128)(2,1)} %constant.83) | copy-start | bytes 98308
  0.6 21.8 %copy-start.17 = (bf16[27,128]{1,0:T(8,128)(2,1)S(1)}, bf16[27,128]{1,0:T(8,128)(2,1)}, u32[]{:S(2)}) copy-start(bf16[27,128]{1,0:T(8,128)(2,1)} %param.19) | copy-start | bytes 20740
  2.1 20.7 %copy-start.19 = (pred[3,72,512]{2,1,0:T(8,128)(4,1)S(1)}, pred[3,72,512]{2,1,0:T(8,128)(4,1)}, u32[]{:S(2)}) copy-start(pred[3,72,512]{2,1,0:T(8,128)(4,1)} %constant.75) | copy-start | bytes 331780
  2.1 20.7 %copy-start.22 = (bf16[72,4,1,1]{0,1,3,2:T(4,128)(2,1)S(1)}, bf16[72,4,1,1]{0,1,3,2:T(4,128)(2,1)}, u32[]{:S(2)}) copy-start(bf16[72,4,1,1]{0,1,3,2:T(4,128)(2,1)} %constant.84) | copy-start | bytes 1732
  30.5 2.6 %copy-start.2 = (bf16[1,2,4,1024]{3,2,1,0:T(4,128)(2,1)S(1)}, bf16[1,2,4,1024]{3,2,1,0:T(4,128)(2,1)}, u32[]{:S(2)}) copy-start(bf16[1,2,4,1024]{3,2,1,0:T(4,128)(2,1)} %param.21) | copy-start | bytes 49156
  30.5 2.6 %copy-start.13 = (bf16[4,1,1024]{2,1,0:T(2,128)(2,1)S(1)}, bf16[4,1,1024]{2,1,0:T(2,128)(2,1)}, u32[]{:S(2)}) copy-start(bf16[4,1,1024]{2,1,0:T(2,128)(2,1)} %get-tuple-element.17) | copy-start | bytes 24580
  30.6 2.6 %copy-start.14 = (bf16[4,1,1024]{2,1,0:T(2,128)(2,1)S(1)}, bf16[4,1,1024]{2,1,0:T(2,128)(2,1)}, u32[]{:S(2)}) copy-start(bf16[4,1,1024]{2,1,0:T(2,128)(2,1)} %get-tuple-element.20) | copy-start | bytes 24580
  30.6 2.6 %copy-start.15 = (bf16[1,4,1024]{2,1,0:T(4,128)(2,1)S(1)}, bf16[1,4,1024]{2,1,0:T(4,128)(2,1)}, u32[]{:S(2)}) copy-start(bf16[1,4,1024]{2,1,0:T(4,128)(2,1)} %get-tuple-element.18) | copy-start | bytes 24580
  30.6 2.6 %copy-start.16 = (bf16[1,4,1024]{2,1,0:T(4,128)(2,1)S(1)}, bf16[1,4,1024]{2,1,0:T(4,128)(2,1)}, u32[]{:S(2)}) copy-start(bf16[1,4,1024]{2,1,0:T(4,128)(2,1)} %get-tuple-element.19) | copy-start | bytes 24580
  31.0 2.5 %copy-start.5 = (bf16[27,2048]{1,0:T(8,128)(2,1)S(1)}, bf16[27,2048]{1,0:T(8,128)(2,1)}, u32[]{:S(2)}) copy-start(bf16[27,2048]{1,0:T(8,128)(2,1)} %param.20) | copy-start | bytes 331780
  31.1 2.5 %copy-start.1 = (pred[3,192,256]{2,1,0:T(32,128)(4,1)S(1)}, pred[3,192,256]{2,1,0:T(32,128)(4,1)}, u32[]{:S(2)}) copy-start(pred[3,192,256]{2,1,0:T(32,128)(4,1)} %constant.76) | copy-start | bytes 442372
  31.3 2.4 %copy-start.20 = (bf16[64,256,1,1]{1,0,3,2:T(8,128)(2,1)S(1)}, bf16[64,256,1,1]{1,0,3,2:T(8,128)(2,1)}, u32[]{:S(2)}) copy-start(bf16[64,256,1,1]{1,0,3,2:T(8,128)(2,1)} %constant.85) | copy-start | bytes 98308
  31.3 2.4 %copy-start.21 = (bf16[192,32,1,1]{0,1,3,2:T(8,128)(2,1)S(1)}, bf16[192,32,1,1]{0,1,3,2:T(8,128)(2,1)}, u32[]{:S(2)}) copy-start(bf16[192,32,1,1]{0,1,3,2:T(8,128)(2,1)} %constant.86) | copy-start | bytes 36868
  36.4 0.8 %copy-start.8 = (pred[6,32,256]{2,1,0:T(32,128)(4,1)S(1)}, pred[6,32,256]{2,1,0:T(32,128)(4,1)}, u32[]{:S(2)}) copy-start(pred[6,32,256]{2,1,0:T(32,128)(4,1)} %constant.80) | copy-start | bytes 147460
  36.4 0.8 %copy-start.7 = (pred[6,32,256]{2,1,0:T(32,128)(4,1)S(1)}, pred[6,32,256]{2,1,0:T(32,128)(4,1)}, u32[]{:S(2)}) copy-start(pred[6,32,256]{2,1,0:T(32,128)(4,1)} %constant.82) | copy-start | bytes 147460
  36.4 0.9 %copy-start.6 = (pred[6,32,256]{2,1,0:T(32,128)(4,1)S(1)}, pred[6,32,256]{2,1,0:T(32,128)(4,1)}, u32[]{:S(2)}) copy-start(pred[6,32,256]{2,1,0:T(32,128)(4,1)} %constant.81) | copy-start | bytes 147460
  37.3 0.9 %copy-start.4 = (f32[256,64]{1,0:T(8,128)S(1)}, f32[256,64]{1,0:T(8,128)}, u32[]{:S(2)}) copy-start(f32[256,64]{1,0:T(8,128)} %constant.56.clone) | copy-start | bytes 196612
  45.0 0.8 copy-start.9
  45.0 0.8 copy-start.10
  45.0 0.8 copy-start.11
  45.8 1.0 %copy-start = (f32[512,32]{1,0:T(8,128)S(1)}, f32[512,32]{1,0:T(8,128)}, u32[]{:S(2)}) copy-start(f32[512,32]{1,0:T(8,128)} %constant.60.clone) | copy-start | bytes 196612
  45.8 30.4 %copy-start.3 = (f32[8,6,10,256]{3,0,2,1:T(8,128)S(1)}, f32[8,6,10,256]{3,0,2,1:T(8,128)}, u32[]{:S(2)}) copy-start(f32[8,6,10,256]{3,0,2,1:T(8,128)} %get-tuple-element.86) | copy-start | bytes 1474564
  76.5 3.0 %copy-start.18 = (bf16[2,4,1024]{2,1,0:T(4,128)(2,1)}, bf16[2,4,1024]{2,1,0:T(4,128)(2,1)S(1)}, u32[]{:S(2)}) copy-start(bf16[2,4,1024]{2,1,0:T(4,128)(2,1)S(1)} %constant_dynamic-update-slice_fusion) | copy-start | bytes 49156

commit v2 on v1

--- a/solution.py
+++ b/solution.py
@@ -11,34 +11,45 @@
 CH_TWO = 64
 
 MESH = pl.DeviceIdType.MESH
-CHUNK = 32
-
-
-def sum_kernel(first, second, first_out, second_out, x_ref, near, part, far, gathered, sends, recvs):
+PART = (4, 8, 128)
+
+
+def sum_kernel(
+    first, second, first_out, second_out, x_ref, near, part, quad, own, deep, spread, gathered, sends, recvs
+):
     row = lax.axis_index("gx")
     column = lax.axis_index("gy")
     sample = lax.axis_index("sa")
     me = column * 4 + sample
+    high = row // 4
+    low = row % 4
     barrier = pltpu.get_barrier_semaphore()
 
     def plane_peer(k):
         other = (me + k) % 16
         return other, (row, other // 4, other % 4)
 
-    def row_peer(k):
-        other = (row + k) % 16
-        return other, (other, column, sample)
-
-    for k in range(1, 16):
-        pl.semaphore_signal(barrier, inc=1, device_id=plane_peer(k)[1], device_id_type=MESH)
-        pl.semaphore_signal(barrier, inc=1, device_id=row_peer(k)[1], device_id_type=MESH)
+    def low_peer(k):
+        other = (low + k) % 4
+        return other, (high * 4 + other, column, sample)
+
+    def high_peer(k):
+        other = (high + k) % 4
+        return other, (other * 4 + low, column, sample)
+
+    for peer, count in ((plane_peer, 16), (low_peer, 4), (high_peer, 4)):
+        for k in range(1, count):
+            pl.semaphore_signal(barrier, inc=1, device_id=peer(k)[1], device_id_type=MESH)
     x_ref[...] = jnp.zeros_like(x_ref)
     for g in range(16):
-        x_ref[g, 0:27] = second[:, 128 * g : 128 * g + 128]
+        lanes = slice(128 * g, 128 * g + 128)
+        for q in range(3):
+            x_ref[g, q] = second[8 * q : 8 * q + 8, lanes]
+        x_ref[g, 3, 0:3] = second[24:27, lanes]
         rows = min(2, 27 - 2 * g)
         if rows > 0:
-            x_ref[g, 27 : 27 + rows] = first[2 * g : 2 * g + rows]
-    pl.semaphore_wait(barrier, 30)
+            x_ref[g, 3, 3 : 3 + rows] = first[2 * g : 2 * g + rows]
+    pl.semaphore_wait(barrier, 21)
 
     def send(stage, k, source, target, device):
         copy = pltpu.make_async_remote_copy(
@@ -61,34 +72,50 @@
         copies[k - 1].wait_recv()
         total = total + near[k]
     part[...] = total
-    far[row] = total
-    second = []
-    for k in range(1, 16):
-        other, device = row_peer(k)
-        second.append(send(1, k, part, far.at[row], device))
-    for copy in second:
+    second_copies = []
+    for k in range(1, 4):
+        other, device = low_peer(k)
+        second_copies.append(send(1, k, part.at[other], quad.at[k], device))
+    total = part[low]
+    for k in range(1, 4):
+        second_copies[k - 1].wait_recv()
+        total = total + quad[k]
+    own[...] = total
+    deep[high] = total
+    third_copies = []
+    for k in range(1, 4):
+        other, device = high_peer(k)
+        third_copies.append(send(2, k, own, deep.at[high], device))
+    for copy in third_copies:
         copy.wait_recv()
-    total = far[0]
-    for k in range(1, 16):
-        total = total + far[k]
-    gathered[me] = total
-    third = []
+    spread[low] = (deep[0] + deep[1]) + (deep[2] + deep[3])
+    fourth_copies = []
+    for k in range(1, 4):
+        other, device = low_peer(k)
+        fourth_copies.append(send(3, k, spread.at[low], spread.at[low], device))
+    for copy in fourth_copies:
+        copy.wait_recv()
+    last_copies = []
     for k in range(1, 16):
         other, device = plane_peer(k)
-        third.append(send(2, k, gathered.at[me], gathered.at[me], device))
-    for copy in third:
+        last_copies.append(send(4, k, spread, gathered.at[me], device))
+    gathered[me] = spread[...]
+    for copy in last_copies:
         copy.wait_recv()
     for g in range(16):
-        second_out[:, 128 * g : 128 * g + 128] = gathered[g, 0:27]
+        lanes = slice(128 * g, 128 * g + 128)
+        for q in range(3):
+            second_out[8 * q : 8 * q + 8, lanes] = gathered[g, q]
+        second_out[24:27, lanes] = gathered[g, 3, 0:3]
         rows = min(2, 27 - 2 * g)
         if rows > 0:
-            first_out[2 * g : 2 * g + rows] = gathered[g, 27 : 27 + rows]
-    for copy in copies + second + third:
+            first_out[2 * g : 2 * g + rows] = gathered[g, 3, 3 : 3 + rows]
+    for copy in copies + second_copies + third_copies + fourth_copies + last_copies:
         copy.wait_send()
 
 
 def sum_over_devices(first, second):
-    block = (16, CHUNK, 128)
+    block = (16,) + PART
     whole = pl.BlockSpec(memory_space=pltpu.VMEM)
     return pl.pallas_call(
         sum_kernel,
@@ -101,19 +128,22 @@
         scratch_shapes=[
             pltpu.VMEM(block, jnp.float32),
             pltpu.VMEM(block, jnp.float32),
-            pltpu.VMEM(block[1:], jnp.float32),
+            pltpu.VMEM(PART, jnp.float32),
+            pltpu.VMEM(PART, jnp.float32),
+            pltpu.VMEM(PART[1:], jnp.float32),
+            pltpu.VMEM(PART, jnp.float32),
+            pltpu.VMEM(PART, jnp.float32),
             pltpu.VMEM(block, jnp.float32),
-            pltpu.VMEM(block, jnp.float32),
-            pltpu.SemaphoreType.DMA((3, 16)),
-            pltpu.SemaphoreType.DMA((3, 16)),
+            pltpu.SemaphoreType.DMA((5, 16)),
+            pltpu.SemaphoreType.DMA((5, 16)),
         ],
         compiler_params=pltpu.CompilerParams(collective_id=0, has_side_effects=True),
         name="sum_over_devices",
     )(first, second)
 
 
-def halo_kernel(volume, low, high, outer, outer_low, outer_high, *refs):
-    outs, slots, sends, recvs = refs[:8], refs[8:16], refs[16], refs[17]
+def halo_kernel(volume, outer, *refs):
+    outs, slots, edges, sends, recvs = refs[:8], refs[8:16], refs[16:20], refs[20], refs[21]
     row = lax.axis_index("gx")
     column = lax.axis_index("gy")
     sample = lax.axis_index("sa")
@@ -127,6 +157,10 @@
     around = [(dx, dy) for dx in (-1, 0, 1) for dy in (-1, 0, 1) if (dx, dy) != (0, 0)]
     for dx, dy in around:
         pl.semaphore_signal(barrier, inc=1, device_id=device(dx, dy), device_id_type=MESH)
+    for whole, first, last in ((volume, *edges[:2]), (outer, *edges[2:])):
+        width = first.shape[1]
+        first[...] = whole[:, :width]
+        last[...] = whole[:, whole.shape[1] - width :]
     pl.semaphore_wait(barrier, 8)
     copies = []
 
@@ -144,8 +178,8 @@
         copies.append(copy)
 
     groups = (
-        (volume, low, high, slots[:4]),
-        (outer, outer_low, outer_high, slots[4:]),
+        (volume, *edges[:2], slots[:4]),
+        (outer, *edges[2:], slots[4:]),
     )
     for whole, first, last, (left, right, top, bottom) in groups:
         size = whole.shape[0]
@@ -170,23 +204,23 @@
 
 
 def exchange(volume, outer):
-    args = []
     shapes = []
+    edges = []
     for x, width in ((volume, 5), (outer, 1)):
         rows, columns, lanes = x.shape
-        args += [x, x[:, :width], x[:, columns - width :]]
+        edges += [(rows, width, lanes)] * 2
         shapes += [(rows + 2 * width, width, lanes)] * 2 + [(width, columns, lanes)] * 2
     space = pl.BlockSpec(memory_space=pltpu.VMEM)
     pieces = pl.pallas_call(
         halo_kernel,
         out_shape=tuple(jax.ShapeDtypeStruct(shape, jnp.bfloat16) for shape in shapes),
-        in_specs=[space] * 6,
+        in_specs=[space] * 2,
         out_specs=(space,) * 8,
-        scratch_shapes=[pltpu.VMEM(shape, jnp.bfloat16) for shape in shapes]
+        scratch_shapes=[pltpu.VMEM(shape, jnp.bfloat16) for shape in shapes + edges]
         + [pltpu.SemaphoreType.DMA((16,)), pltpu.SemaphoreType.DMA((16,))],
         compiler_params=pltpu.CompilerParams(collective_id=1, has_side_effects=True),
         name="exchange",
-    )(*args)
+    )(volume, outer)
     result = []
     for x, (left, right, top, bottom) in ((volume, pieces[:4]), (outer, pieces[4:])):
         middle = jnp.concatenate([top, x, bottom], axis=0)

time: 80.1 us -> 79.4 us (level)
  local copies, waits for them, and re-layouts: 13.6 us -> 10.8 us
  Pallas kernels: 45.7 us -> 47.9 us
    slice x2 -> x0, local copies, waits for them, and re-layouts: 2.82 us -> none  [exchange(): args += [x, x[:, :width], x[:, columns - width:]]]
    pallas_call x1, Pallas kernels: 28.3 us -> 30.4 us  [sum_over_devices(): pl.pallas_call(sum_kernel, out_shape=(jax.ShapeDtypeStruct(first.shape, j...]
where the time goes in v2:
time: 79.4 us; the launch traced here: 78.9 us
  Pallas kernels  47.9 us (60%)
  matrix products  14.4 us (18%)
  local copies, waits for them, and re-layouts  10.8 us (14%)
  other arithmetic  4.23 us (5%)
  between operations  1.52 us (2%)
    pallas_call x1, Pallas kernels, sum_over_devices(): pl.pallas_call(sum_kernel, out_shape=(jax.ShapeDtypeStruct(first.shape, j...  30.4 us
    pallas_call x1, Pallas kernels, exchange(): pl.pallas_call(halo_kernel, out_shape=tuple((jax.ShapeDtypeStruct(shape,...  17.5 us
    conv_general_dilated x3, matrix products, convolve(): lax.conv_general_dilated(padded, weight, (1, 1), padding, dimension_numbe...  7.62 us
    unnamed x88, local copies, waits for them, and re-layouts  4.97 us
    conv_general_dilated x2, matrix products, weight_gradient(): lax.conv_general_dilated(padded, grad, (1, 1), 'VALID', dimension_numbers...  3.59 us
    another operation x11, local copies, waits for them, and re-layouts, chunks(): jnp.stack([values[..., j * step:j * step + width] for j in range(count)])  2.27 us
    dot_general x2, matrix products, banded(): jnp.einsum('ri,kcin->kcrn', spread_rows, wide, preferred_element_type=jnp...  1.84 us

profile of v2, /device:TPU:1, one launch (start us, length us, event | category | flops | bytes accessed | tf_op | source)
XLA Modules:
  0.0 78.9 jit_solution(2684098333725399669)
XLA Ops:
  0.7 17.5 %exchange.1 = (bf16[18,5,256]{2,1,0:T(8,128)(2,1)}, bf16[18,5,256]{2,1,0:T(8,128)(2,1)}, bf16[5,16,256]{2,1,0:T(8,128)(2,1)}, bf16[5,16,256]{2,1,0:T(8,128)(2,1)...) custom-call(bf16[8,16,256]{2,1,0:T(8,128)(2,1)} %bitcast.241, ...), custom_call_target="tpu_custom_call" | custom-call | tf_op jit(solution)/shard_map/exchange/pallas_call | solution.py:214
  18.2 1.1 %pad_maximum_fusion.2 = bf16[18,26,256]{2,1,0:T(8,128)(2,1)S(1)} fusion(bf16[18,5,256]{2,1,0:T(8,128)(2,1)} %get-tuple-element.16, bf16[5,16,256]{2,1,0:T(8,128)(2,1)} %get-tuple-element.15, bf16[8,16,256]{2,1,0:T(8,128)(2,1)} %bitcast.242, bf16[5,16,256]{2,1,0:T(8,128)(2,1)} %get-tuple-element.14, bf16[18,5,256]{2,1,0:T(8,128)(2,1)} %get-tuple-element.13), kind=kLoop, calls=%fused_computation.29 | loop fusion | flops 1198080 | bytes 479232 | tf_op jit(solution)/shard_map/concatenate | solution.py:227
  19.3 0.2 fusion.12
  19.6 0.2 pad_maximum_fusion.1
  19.9 0.2 convolution_bitcast_fusion.1
  20.1 0.8 fusion.1
  20.8 5.6 %divide_multiply_fusion = (f32[4,16,24,512]{3,0,2,1:T(4,128)S(1)}, f32[4,16,24,512]{3,0,2,1:T(4,128)}) fusion(bf16[3,3,72,512]{3,2,1,0:T(8,128)(2,1)S(1)} %bitcast.265, bf16[4,18,26,72]{3,2,1,0:T(8,128)(2,1)S(1)} %pad_maximum_fusion.1), kind=kOutput, calls=%fused_computation | convolution fusion | flops 1022361600 | bytes 7224576 | tf_op jit(solution)/shard_map/conv_general_dilated | solution.py:275
  26.5 0.4 slice_add_fusion
  26.9 0.4 reduce_sum.91
  27.5 0.3 fusion.40
  27.9 0.2 fusion.23
  29.0 1.4 %stack.121 = bf16[8,8,12,192]{3,0,2,1:T(8,128)(2,1)S(1)} concatenate(bf16[1,8,12,192]{3,0,2,1:T(2,128)(2,1)S(1)} %copy.679, bf16[1,8,12,192]{3,0,2,1:T(2,128)(2,1)S(1)} %copy.680, bf16[1,8,12,192]{3,0,2,1:T(2,128)(2,1)S(1)} %copy.681, bf16[1,8,12,192]{3,0,2,1:T(2,128)(2,1)S(1)} %copy.682, bf16[1,8,12,192]{3,0,2,1:T(2,128)(2,1)S(1)} %copy.683, bf16[1,8,12,192]{3,0,2,1:T(2,128)(2,1)S(1)} %copy.684, ...), dimensions={0} | concatenate | bytes 589824 | tf_op jit(solution)/shard_map/stack | solution.py:311
  30.8 0.2 dot_general.25
  31.1 1.1 %fusion = bf16[9,192,256]{2,1,0:T(8,128)(2,1)S(1)} fusion(pred[3,192,256]{2,1,0:T(8,128)(4,1)S(1)} %copy.797, bf16[192,32,1,1]{0,1,3,2:T(8,128)(2,1)S(1)} %copy-done.21, bf16[64,256,1,1]{1,0,3,2:T(8,128)(2,1)S(1)} %copy-done.20, bf16[9,3,32,64]{3,2,1,0:T(8,128)(2,1)S(1)} %dot_general.25), kind=kOutput, calls=%fused_computation.2 | convolution fusion | flops 115458048 | bytes 1187840 | tf_op jit(solution)/shard_map/ri,kcin->kcrn/dot_general | solution.py:254
  32.2 1.5 %multiply_convert_fusion = (bf16[8,6,10,256]{3,0,2,1:T(8,128)(2,1)S(1)}, f32[8,6,10,256]{3,0,2,1:T(8,128)}) fusion(bf16[8,8,12,128]{3,0,2,1:T(8,128)(2,1)S(1)} %bitcast.243, bf16[8,8,12,192]{3,0,2,1:T(8,128)(2,1)S(1)} %stack.121, bf16[3,3,192,256]{3,2,1,0:T(8,128)(2,1)S(1)} %bitcast.263), kind=kOutput, calls=%fused_computation.21 | convolution fusion | flops 426393600 | bytes 2113536 | tf_op jit(solution)/shard_map/conv_general_dilated | solution.py:275
  33.7 0.6 fusion.14
  34.2 0.2 copy-done.8
  34.6 0.4 select_reduce_fusion.2
  35.0 0.4 copy-done.3
  35.5 0.9 %fusion.44 = f32[864,64]{1,0:T(8,128)S(1)} fusion(f32[864,256]{1,0:T(8,128)S(1)} %bitcast.229, f32[256,64]{1,0:T(8,128)S(1)} %copy-done.3), kind=kOutput, calls=%fused_computation.160 | convolution fusion | flops 169869312 | bytes 1171456 | tf_op jit(solution)/shard_map/dot_general | solution.py:265
  36.3 0.9 %reshape.69.second = f32[27,2048]{1,0:T(8,128)} reshape(f32[864,64]{1,0:T(8,128)S(1)} %fusion.44) | data formatting | bytes 442368 | tf_op jit(solution)/shard_map/reshape | solution.py:271
  37.2 0.5 fusion.42
  38.3 0.3 fusion.39
  39.3 3.0 %fusion.3 = f32[3,3,72,512]{3,2,1,0:T(8,128)S(1)} fusion(f32[4,8,16,256]{3,0,2,1:T(4,128)S(1)} %bitcast.236, f32[4,16,24,512]{3,0,2,1:T(4,128)} %get-tuple-element.80, bf16[4,18,26,72]{3,2,1,0:T(8,128)(2,1)S(1)} %pad_maximum_fusion.1), kind=kOutput, calls=%fused_computation.20 | convolution fusion | flops 342622208 | bytes 3169536 | tf_op jit(solution)/shard_map/conv_general_dilated | solution.py:286
  42.3 0.4 reshape.64
  42.7 0.3 copy-done.9
  43.1 0.9 %select_reduce_fusion.5 = (f32[9,4,512]{2,1,0:T(4,128)S(1)}, f32[9,4,512]{2,1,0:T(4,128)S(1)}, f32[9,4,512]{2,1,0:T(4,128)S(1)}) fusion(f32[9,18,4,512]{3,2,1,0:T(4,128)S(1)} %reshape.64, pred[18,4,512]{2,1,0:T(4,128)(4,1)S(1)} %copy-done.9, pred[18,4,512]{2,1,0:T(4,128)(4,1)S(1)} %copy-done.11, pred[18,4,512]{2,1,0:T(4,128)(4,1)S(1)} %copy-done.10), kind=kLoop, calls=%fused_computation.11 | loop fusion | flops 1935360 | bytes 1658880 | tf_op jit(solution)/shard_map/reduce_sum | solution.py:263
  44.1 0.4 fusion.43
  44.5 0.7 reshape.66.first
  45.2 30.4 %sum_over_devices.1 = (f32[27,128]{1,0:T(8,128)}, f32[27,2048]{1,0:T(8,128)}) custom-call(f32[27,128]{1,0:T(8,128)} %reshape.66.first, f32[27,2048]{1,0:T(8,128)} %reshape.69.second), custom_call_target="tpu_custom_call" | custom-call | tf_op jit(solution)/shard_map/sum_over_devices/pallas_call | solution.py:120
  75.9 1.3 %copy.801 = f32[27,128]{1,0:T(8,128)} copy(f32[27,128]{1,0:T(8,128)} %get-tuple-element.91) | data formatting | bytes 27648
  77.2 1.7 %copy.802 = f32[27,2048]{1,0:T(8,128)} copy(f32[27,2048]{1,0:T(8,128)} %get-tuple-element.92) | data formatting | bytes 442368
  (122 shorter events, 3.0 us)
Async XLA Ops:
  0.6 19.2 %copy-start.12 = (bf16[32,512,1,1]{1,0,3,2:T(8,128)(2,1)S(1)}, bf16[32,512,1,1]{1,0,3,2:T(8,128)(2,1)}, u32[]{:S(2)}) copy-start(bf16[32,512,1,1]{1,0,3,2:T(8,128)(2,1)} %constant.83) | copy-start | bytes 98308
  0.6 19.4 %copy-start.19 = (pred[3,72,512]{2,1,0:T(8,128)(4,1)S(1)}, pred[3,72,512]{2,1,0:T(8,128)(4,1)}, u32[]{:S(2)}) copy-start(pred[3,72,512]{2,1,0:T(8,128)(4,1)} %constant.75) | copy-start | bytes 331780
  0.7 19.4 %copy-start.22 = (bf16[72,4,1,1]{0,1,3,2:T(4,128)(2,1)S(1)}, bf16[72,4,1,1]{0,1,3,2:T(4,128)(2,1)}, u32[]{:S(2)}) copy-start(bf16[72,4,1,1]{0,1,3,2:T(4,128)(2,1)} %constant.84) | copy-start | bytes 1732
  0.7 19.1 %copy-start.17 = (bf16[27,128]{1,0:T(8,128)(2,1)S(1)}, bf16[27,128]{1,0:T(8,128)(2,1)}, u32[]{:S(2)}) copy-start(bf16[27,128]{1,0:T(8,128)(2,1)} %param.19) | copy-start | bytes 20740
  27.9 2.6 %copy-start.5 = (bf16[1,2,4,1024]{3,2,1,0:T(4,128)(2,1)S(1)}, bf16[1,2,4,1024]{3,2,1,0:T(4,128)(2,1)}, u32[]{:S(2)}) copy-start(bf16[1,2,4,1024]{3,2,1,0:T(4,128)(2,1)} %param.21) | copy-start | bytes 49156
  27.9 2.6 %copy-start.13 = (bf16[4,1,1024]{2,1,0:T(2,128)(2,1)S(1)}, bf16[4,1,1024]{2,1,0:T(2,128)(2,1)}, u32[]{:S(2)}) copy-start(bf16[4,1,1024]{2,1,0:T(2,128)(2,1)} %get-tuple-element.17) | copy-start | bytes 24580
  27.9 2.6 %copy-start.14 = (bf16[4,1,1024]{2,1,0:T(2,128)(2,1)S(1)}, bf16[4,1,1024]{2,1,0:T(2,128)(2,1)}, u32[]{:S(2)}) copy-start(bf16[4,1,1024]{2,1,0:T(2,128)(2,1)} %get-tuple-element.20) | copy-start | bytes 24580
  27.9 2.6 %copy-start.15 = (bf16[1,4,1024]{2,1,0:T(4,128)(2,1)S(1)}, bf16[1,4,1024]{2,1,0:T(4,128)(2,1)}, u32[]{:S(2)}) copy-start(bf16[1,4,1024]{2,1,0:T(4,128)(2,1)} %get-tuple-element.18) | copy-start | bytes 24580
  27.9 2.6 %copy-start.16 = (bf16[1,4,1024]{2,1,0:T(4,128)(2,1)S(1)}, bf16[1,4,1024]{2,1,0:T(4,128)(2,1)}, u32[]{:S(2)}) copy-start(bf16[1,4,1024]{2,1,0:T(4,128)(2,1)} %get-tuple-element.19) | copy-start | bytes 24580
  28.3 2.5 %copy-start.4 = (bf16[27,2048]{1,0:T(8,128)(2,1)S(1)}, bf16[27,2048]{1,0:T(8,128)(2,1)}, u32[]{:S(2)}) copy-start(bf16[27,2048]{1,0:T(8,128)(2,1)} %param.20) | copy-start | bytes 331780
  28.5 2.5 %copy-start.1 = (pred[3,192,256]{2,1,0:T(32,128)(4,1)S(1)}, pred[3,192,256]{2,1,0:T(32,128)(4,1)}, u32[]{:S(2)}) copy-start(pred[3,192,256]{2,1,0:T(32,128)(4,1)} %constant.76) | copy-start | bytes 442372
  28.7 2.4 %copy-start.20 = (bf16[64,256,1,1]{1,0,3,2:T(8,128)(2,1)S(1)}, bf16[64,256,1,1]{1,0,3,2:T(8,128)(2,1)}, u32[]{:S(2)}) copy-start(bf16[64,256,1,1]{1,0,3,2:T(8,128)(2,1)} %constant.85) | copy-start | bytes 98308
  28.7 2.4 %copy-start.21 = (bf16[192,32,1,1]{0,1,3,2:T(8,128)(2,1)S(1)}, bf16[192,32,1,1]{0,1,3,2:T(8,128)(2,1)}, u32[]{:S(2)}) copy-start(bf16[192,32,1,1]{0,1,3,2:T(8,128)(2,1)} %constant.86) | copy-start | bytes 36868
  33.7 0.8 %copy-start.8 = (pred[6,32,256]{2,1,0:T(32,128)(4,1)S(1)}, pred[6,32,256]{2,1,0:T(32,128)(4,1)}, u32[]{:S(2)}) copy-start(pred[6,32,256]{2,1,0:T(32,128)(4,1)} %constant.80) | copy-start | bytes 147460
  33.7 0.8 %copy-start.7 = (pred[6,32,256]{2,1,0:T(32,128)(4,1)S(1)}, pred[6,32,256]{2,1,0:T(32,128)(4,1)}, u32[]{:S(2)}) copy-start(pred[6,32,256]{2,1,0:T(32,128)(4,1)} %constant.82) | copy-start | bytes 147460
  33.7 0.9 %copy-start.6 = (pred[6,32,256]{2,1,0:T(32,128)(4,1)S(1)}, pred[6,32,256]{2,1,0:T(32,128)(4,1)}, u32[]{:S(2)}) copy-start(pred[6,32,256]{2,1,0:T(32,128)(4,1)} %constant.81) | copy-start | bytes 147460
  34.6 0.9 %copy-start.3 = (f32[256,64]{1,0:T(8,128)S(1)}, f32[256,64]{1,0:T(8,128)}, u32[]{:S(2)}) copy-start(f32[256,64]{1,0:T(8,128)} %constant.56.clone) | copy-start | bytes 196612
  42.3 0.8 copy-start.9
  42.3 0.8 copy-start.10
  42.3 0.8 copy-start.11
  43.1 1.0 %copy-start = (f32[512,32]{1,0:T(8,128)S(1)}, f32[512,32]{1,0:T(8,128)}, u32[]{:S(2)}) copy-start(f32[512,32]{1,0:T(8,128)} %constant.60.clone) | copy-start | bytes 196612
  43.1 32.5 %copy-start.2 = (f32[8,6,10,256]{3,0,2,1:T(8,128)S(1)}, f32[8,6,10,256]{3,0,2,1:T(8,128)}, u32[]{:S(2)}) copy-start(f32[8,6,10,256]{3,0,2,1:T(8,128)} %get-tuple-element.82) | copy-start | bytes 1474564
  75.9 3.0 %copy-start.18 = (bf16[2,4,1024]{2,1,0:T(4,128)(2,1)}, bf16[2,4,1024]{2,1,0:T(4,128)(2,1)S(1)}, u32[]{:S(2)}) copy-start(bf16[2,4,1024]{2,1,0:T(4,128)(2,1)S(1)} %constant_dynamic-update-slice_fusion) | copy-start | bytes 49156

commit v3 on v1

--- a/solution.py
+++ b/solution.py
@@ -112,8 +112,8 @@
     )(first, second)
 
 
-def halo_kernel(volume, low, high, outer, outer_low, outer_high, *refs):
-    outs, slots, sends, recvs = refs[:8], refs[8:16], refs[16], refs[17]
+def halo_kernel(volume, outer, *refs):
+    outs, slots, edges, sends, recvs = refs[:8], refs[8:16], refs[16:20], refs[20], refs[21]
     row = lax.axis_index("gx")
     column = lax.axis_index("gy")
     sample = lax.axis_index("sa")
@@ -127,6 +127,10 @@
     around = [(dx, dy) for dx in (-1, 0, 1) for dy in (-1, 0, 1) if (dx, dy) != (0, 0)]
     for dx, dy in around:
         pl.semaphore_signal(barrier, inc=1, device_id=device(dx, dy), device_id_type=MESH)
+    for whole, first, last in ((volume, *edges[:2]), (outer, *edges[2:])):
+        width = first.shape[1]
+        first[...] = whole[:, :width]
+        last[...] = whole[:, whole.shape[1] - width :]
     pl.semaphore_wait(barrier, 8)
     copies = []
 
@@ -144,8 +148,8 @@
         copies.append(copy)
 
     groups = (
-        (volume, low, high, slots[:4]),
-        (outer, outer_low, outer_high, slots[4:]),
+        (volume, *edges[:2], slots[:4]),
+        (outer, *edges[2:], slots[4:]),
     )
     for whole, first, last, (left, right, top, bottom) in groups:
         size = whole.shape[0]
@@ -170,23 +174,23 @@
 
 
 def exchange(volume, outer):
-    args = []
     shapes = []
+    edges = []
     for x, width in ((volume, 5), (outer, 1)):
         rows, columns, lanes = x.shape
-        args += [x, x[:, :width], x[:, columns - width :]]
+        edges += [(rows, width, lanes)] * 2
         shapes += [(rows + 2 * width, width, lanes)] * 2 + [(width, columns, lanes)] * 2
     space = pl.BlockSpec(memory_space=pltpu.VMEM)
     pieces = pl.pallas_call(
         halo_kernel,
         out_shape=tuple(jax.ShapeDtypeStruct(shape, jnp.bfloat16) for shape in shapes),
-        in_specs=[space] * 6,
+        in_specs=[space] * 2,
         out_specs=(space,) * 8,
-        scratch_shapes=[pltpu.VMEM(shape, jnp.bfloat16) for shape in shapes]
+        scratch_shapes=[pltpu.VMEM(shape, jnp.bfloat16) for shape in shapes + edges]
         + [pltpu.SemaphoreType.DMA((16,)), pltpu.SemaphoreType.DMA((16,))],
         compiler_params=pltpu.CompilerParams(collective_id=1, has_side_effects=True),
         name="exchange",
-    )(*args)
+    )(volume, outer)
     result = []
     for x, (left, right, top, bottom) in ((volume, pieces[:4]), (outer, pieces[4:])):
         middle = jnp.concatenate([top, x, bottom], axis=0)

time: 80.1 us -> 77.3 us (0.965)
  local copies, waits for them, and re-layouts: 13.6 us -> 10.8 us
    slice x2 -> x0, local copies, waits for them, and re-layouts: 2.82 us -> none  [exchange(): args += [x, x[:, :width], x[:, columns - width:]]]
where the time goes in v3:
time: 77.3 us; the launch traced here: 76.8 us
  Pallas kernels  45.9 us (59%)
  matrix products  14.4 us (19%)
  local copies, waits for them, and re-layouts  10.8 us (14%)
  other arithmetic  4.23 us (5%)
  between operations  1.52 us (2%)
    pallas_call x1, Pallas kernels, sum_over_devices(): pl.pallas_call(sum_kernel, out_shape=(jax.ShapeDtypeStruct(first.shape, j...  28.3 us
    pallas_call x1, Pallas kernels, exchange(): pl.pallas_call(halo_kernel, out_shape=tuple((jax.ShapeDtypeStruct(shape,...  17.5 us
    conv_general_dilated x3, matrix products, convolve(): lax.conv_general_dilated(padded, weight, (1, 1), padding, dimension_numbe...  7.62 us
    unnamed x88, local copies, waits for them, and re-layouts  4.97 us
    conv_general_dilated x2, matrix products, weight_gradient(): lax.conv_general_dilated(padded, grad, (1, 1), 'VALID', dimension_numbers...  3.59 us
    another operation x11, local copies, waits for them, and re-layouts, chunks(): jnp.stack([values[..., j * step:j * step + width] for j in range(count)])  2.27 us
    dot_general x2, matrix products, banded(): jnp.einsum('ri,kcin->kcrn', spread_rows, wide, preferred_element_type=jnp...  1.84 us
    reshape x2, local copies, waits for them, and re-layouts, unbanded(): return narrow.reshape(27, inputs * outputs)  1.55 us

profile of v3, /device:TPU:1, one launch (start us, length us, event | category | flops | bytes accessed | tf_op | source)
XLA Modules:
  0.0 76.8 jit_solution(7291639423461995074)
XLA Ops:
  0.7 17.5 %exchange.1 = (bf16[18,5,256]{2,1,0:T(8,128)(2,1)}, bf16[18,5,256]{2,1,0:T(8,128)(2,1)}, bf16[5,16,256]{2,1,0:T(8,128)(2,1)}, bf16[5,16,256]{2,1,0:T(8,128)(2,1)...) custom-call(bf16[8,16,256]{2,1,0:T(8,128)(2,1)} %bitcast.241, ...), custom_call_target="tpu_custom_call" | custom-call | tf_op jit(solution)/shard_map/exchange/pallas_call | solution.py:184
  18.2 1.1 %pad_maximum_fusion.2 = bf16[18,26,256]{2,1,0:T(8,128)(2,1)S(1)} fusion(bf16[18,5,256]{2,1,0:T(8,128)(2,1)} %get-tuple-element.16, bf16[5,16,256]{2,1,0:T(8,128)(2,1)} %get-tuple-element.15, bf16[8,16,256]{2,1,0:T(8,128)(2,1)} %bitcast.242, bf16[5,16,256]{2,1,0:T(8,128)(2,1)} %get-tuple-element.14, bf16[18,5,256]{2,1,0:T(8,128)(2,1)} %get-tuple-element.13), kind=kLoop, calls=%fused_computation.29 | loop fusion | flops 1198080 | bytes 479232 | tf_op jit(solution)/shard_map/concatenate | solution.py:197
  19.3 0.2 fusion.12
  19.6 0.2 pad_maximum_fusion.1
  19.9 0.2 convolution_bitcast_fusion.1
  20.1 0.8 %fusion.1 = bf16[9,72,512]{2,1,0:T(8,128)(2,1)S(1)} fusion(pred[3,72,512]{2,1,0:T(8,128)(4,1)S(1)} %copy-done.19, bf16[72,4,1,1]{0,1,3,2:T(4,128)(2,1)S(1)} %copy-done.22, bf16[9,3,4,512]{3,0,2,1:T(8,128)(2,1)S(1)} %convolution_bitcast_fusion.1), kind=kOutput, calls=%fused_computation.4 | convolution fusion | flops 9621504 | bytes 885312 | tf_op jit(solution)/shard_map/ri,kcin->kcrn/dot_general | solution.py:224
  20.8 5.6 %divide_multiply_fusion = (f32[4,16,24,512]{3,0,2,1:T(4,128)S(1)}, f32[4,16,24,512]{3,0,2,1:T(4,128)}) fusion(bf16[3,3,72,512]{3,2,1,0:T(8,128)(2,1)S(1)} %bitcast.265, bf16[4,18,26,72]{3,2,1,0:T(8,128)(2,1)S(1)} %pad_maximum_fusion.1), kind=kOutput, calls=%fused_computation | convolution fusion | flops 1022361600 | bytes 7224576 | tf_op jit(solution)/shard_map/conv_general_dilated | solution.py:245
  26.5 0.4 slice_add_fusion
  26.9 0.4 reduce_sum.91
  27.5 0.3 fusion.40
  27.9 0.2 fusion.23
  29.0 1.4 %stack.121 = bf16[8,8,12,192]{3,0,2,1:T(8,128)(2,1)S(1)} concatenate(bf16[1,8,12,192]{3,0,2,1:T(2,128)(2,1)S(1)} %copy.679, bf16[1,8,12,192]{3,0,2,1:T(2,128)(2,1)S(1)} %copy.680, bf16[1,8,12,192]{3,0,2,1:T(2,128)(2,1)S(1)} %copy.681, bf16[1,8,12,192]{3,0,2,1:T(2,128)(2,1)S(1)} %copy.682, bf16[1,8,12,192]{3,0,2,1:T(2,128)(2,1)S(1)} %copy.683, bf16[1,8,12,192]{3,0,2,1:T(2,128)(2,1)S(1)} %copy.684, ...), dimensions={0} | concatenate | bytes 589824 | tf_op jit(solution)/shard_map/stack | solution.py:281
  30.8 0.2 dot_general.25
  31.1 1.1 %fusion = bf16[9,192,256]{2,1,0:T(8,128)(2,1)S(1)} fusion(pred[3,192,256]{2,1,0:T(8,128)(4,1)S(1)} %copy.797, bf16[192,32,1,1]{0,1,3,2:T(8,128)(2,1)S(1)} %copy-done.21, bf16[64,256,1,1]{1,0,3,2:T(8,128)(2,1)S(1)} %copy-done.20, bf16[9,3,32,64]{3,2,1,0:T(8,128)(2,1)S(1)} %dot_general.25), kind=kOutput, calls=%fused_computation.2 | convolution fusion | flops 115458048 | bytes 1187840 | tf_op jit(solution)/shard_map/ri,kcin->kcrn/dot_general | solution.py:224
  32.2 1.5 %multiply_convert_fusion = (bf16[8,6,10,256]{3,0,2,1:T(8,128)(2,1)S(1)}, f32[8,6,10,256]{3,0,2,1:T(8,128)}) fusion(bf16[8,8,12,128]{3,0,2,1:T(8,128)(2,1)S(1)} %bitcast.243, bf16[8,8,12,192]{3,0,2,1:T(8,128)(2,1)S(1)} %stack.121, bf16[3,3,192,256]{3,2,1,0:T(8,128)(2,1)S(1)} %bitcast.263), kind=kOutput, calls=%fused_computation.21 | convolution fusion | flops 426393600 | bytes 2113536 | tf_op jit(solution)/shard_map/conv_general_dilated | solution.py:245
  33.7 0.6 fusion.14
  34.2 0.2 copy-done.8
  34.6 0.4 select_reduce_fusion.2
  35.0 0.4 copy-done.3
  35.5 0.9 %fusion.44 = f32[864,64]{1,0:T(8,128)S(1)} fusion(f32[864,256]{1,0:T(8,128)S(1)} %bitcast.229, f32[256,64]{1,0:T(8,128)S(1)} %copy-done.3), kind=kOutput, calls=%fused_computation.160 | convolution fusion | flops 169869312 | bytes 1171456 | tf_op jit(solution)/shard_map/dot_general | solution.py:235
  36.3 0.9 %reshape.69.second = f32[27,2048]{1,0:T(8,128)} reshape(f32[864,64]{1,0:T(8,128)S(1)} %fusion.44) | data formatting | bytes 442368 | tf_op jit(solution)/shard_map/reshape | solution.py:241
  37.2 0.5 fusion.42
  38.3 0.3 fusion.39
  39.3 3.0 %fusion.3 = f32[3,3,72,512]{3,2,1,0:T(8,128)S(1)} fusion(f32[4,8,16,256]{3,0,2,1:T(4,128)S(1)} %bitcast.236, f32[4,16,24,512]{3,0,2,1:T(4,128)} %get-tuple-element.80, bf16[4,18,26,72]{3,2,1,0:T(8,128)(2,1)S(1)} %pad_maximum_fusion.1), kind=kOutput, calls=%fused_computation.20 | convolution fusion | flops 342622208 | bytes 3169536 | tf_op jit(solution)/shard_map/conv_general_dilated | solution.py:256
  42.3 0.4 reshape.64
  42.7 0.3 copy-done.9
  43.1 0.9 %select_reduce_fusion.5 = (f32[9,4,512]{2,1,0:T(4,128)S(1)}, f32[9,4,512]{2,1,0:T(4,128)S(1)}, f32[9,4,512]{2,1,0:T(4,128)S(1)}) fusion(f32[9,18,4,512]{3,2,1,0:T(4,128)S(1)} %reshape.64, pred[18,4,512]{2,1,0:T(4,128)(4,1)S(1)} %copy-done.9, pred[18,4,512]{2,1,0:T(4,128)(4,1)S(1)} %copy-done.11, pred[18,4,512]{2,1,0:T(4,128)(4,1)S(1)} %copy-done.10), kind=kLoop, calls=%fused_computation.11 | loop fusion | flops 1935360 | bytes 1658880 | tf_op jit(solution)/shard_map/reduce_sum | solution.py:233
  44.1 0.4 fusion.43
  44.5 0.7 reshape.66.first
  45.2 28.3 %sum_over_devices.1 = (f32[27,128]{1,0:T(8,128)}, f32[27,2048]{1,0:T(8,128)}) custom-call(f32[27,128]{1,0:T(8,128)} %reshape.66.first, f32[27,2048]{1,0:T(8,128)} %reshape.69.second), custom_call_target="tpu_custom_call" | custom-call | tf_op jit(solution)/shard_map/sum_over_devices/pallas_call | solution.py:93
  73.8 1.3 %copy.801 = f32[27,128]{1,0:T(8,128)} copy(f32[27,128]{1,0:T(8,128)} %get-tuple-element.91) | data formatting | bytes 27648
  75.2 1.7 %copy.802 = f32[27,2048]{1,0:T(8,128)} copy(f32[27,2048]{1,0:T(8,128)} %get-tuple-element.92) | data formatting | bytes 442368
  (122 shorter events, 3.0 us)
Async XLA Ops:
  0.6 19.2 %copy-start.12 = (bf16[32,512,1,1]{1,0,3,2:T(8,128)(2,1)S(1)}, bf16[32,512,1,1]{1,0,3,2:T(8,128)(2,1)}, u32[]{:S(2)}) copy-start(bf16[32,512,1,1]{1,0,3,2:T(8,128)(2,1)} %constant.83) | copy-start | bytes 98308
  0.6 19.4 %copy-start.19 = (pred[3,72,512]{2,1,0:T(8,128)(4,1)S(1)}, pred[3,72,512]{2,1,0:T(8,128)(4,1)}, u32[]{:S(2)}) copy-start(pred[3,72,512]{2,1,0:T(8,128)(4,1)} %constant.75) | copy-start | bytes 331780
  0.7 19.4 %copy-start.22 = (bf16[72,4,1,1]{0,1,3,2:T(4,128)(2,1)S(1)}, bf16[72,4,1,1]{0,1,3,2:T(4,128)(2,1)}, u32[]{:S(2)}) copy-start(bf16[72,4,1,1]{0,1,3,2:T(4,128)(2,1)} %constant.84) | copy-start | bytes 1732
  0.7 19.1 %copy-start.17 = (bf16[27,128]{1,0:T(8,128)(2,1)S(1)}, bf16[27,128]{1,0:T(8,128)(2,1)}, u32[]{:S(2)}) copy-start(bf16[27,128]{1,0:T(8,128)(2,1)} %param.19) | copy-start | bytes 20740
  27.9 2.6 %copy-start.5 = (bf16[1,2,4,1024]{3,2,1,0:T(4,128)(2,1)S(1)}, bf16[1,2,4,1024]{3,2,1,0:T(4,128)(2,1)}, u32[]{:S(2)}) copy-start(bf16[1,2,4,1024]{3,2,1,0:T(4,128)(2,1)} %param.21) | copy-start | bytes 49156
  27.9 2.6 %copy-start.13 = (bf16[4,1,1024]{2,1,0:T(2,128)(2,1)S(1)}, bf16[4,1,1024]{2,1,0:T(2,128)(2,1)}, u32[]{:S(2)}) copy-start(bf16[4,1,1024]{2,1,0:T(2,128)(2,1)} %get-tuple-element.17) | copy-start | bytes 24580
  27.9 2.6 %copy-start.14 = (bf16[4,1,1024]{2,1,0:T(2,128)(2,1)S(1)}, bf16[4,1,1024]{2,1,0:T(2,128)(2,1)}, u32[]{:S(2)}) copy-start(bf16[4,1,1024]{2,1,0:T(2,128)(2,1)} %get-tuple-element.20) | copy-start | bytes 24580
  27.9 2.6 %copy-start.15 = (bf16[1,4,1024]{2,1,0:T(4,128)(2,1)S(1)}, bf16[1,4,1024]{2,1,0:T(4,128)(2,1)}, u32[]{:S(2)}) copy-start(bf16[1,4,1024]{2,1,0:T(4,128)(2,1)} %get-tuple-element.18) | copy-start | bytes 24580
  27.9 2.6 %copy-start.16 = (bf16[1,4,1024]{2,1,0:T(4,128)(2,1)S(1)}, bf16[1,4,1024]{2,1,0:T(4,128)(2,1)}, u32[]{:S(2)}) copy-start(bf16[1,4,1024]{2,1,0:T(4,128)(2,1)} %get-tuple-element.19) | copy-start | bytes 24580
  28.3 2.5 %copy-start.4 = (bf16[27,2048]{1,0:T(8,128)(2,1)S(1)}, bf16[27,2048]{1,0:T(8,128)(2,1)}, u32[]{:S(2)}) copy-start(bf16[27,2048]{1,0:T(8,128)(2,1)} %param.20) | copy-start | bytes 331780
  28.5 2.5 %copy-start.1 = (pred[3,192,256]{2,1,0:T(32,128)(4,1)S(1)}, pred[3,192,256]{2,1,0:T(32,128)(4,1)}, u32[]{:S(2)}) copy-start(pred[3,192,256]{2,1,0:T(32,128)(4,1)} %constant.76) | copy-start | bytes 442372
  28.7 2.4 %copy-start.20 = (bf16[64,256,1,1]{1,0,3,2:T(8,128)(2,1)S(1)}, bf16[64,256,1,1]{1,0,3,2:T(8,128)(2,1)}, u32[]{:S(2)}) copy-start(bf16[64,256,1,1]{1,0,3,2:T(8,128)(2,1)} %constant.85) | copy-start | bytes 98308
  28.7 2.4 %copy-start.21 = (bf16[192,32,1,1]{0,1,3,2:T(8,128)(2,1)S(1)}, bf16[192,32,1,1]{0,1,3,2:T(8,128)(2,1)}, u32[]{:S(2)}) copy-start(bf16[192,32,1,1]{0,1,3,2:T(8,128)(2,1)} %constant.86) | copy-start | bytes 36868
  33.7 0.8 %copy-start.8 = (pred[6,32,256]{2,1,0:T(32,128)(4,1)S(1)}, pred[6,32,256]{2,1,0:T(32,128)(4,1)}, u32[]{:S(2)}) copy-start(pred[6,32,256]{2,1,0:T(32,128)(4,1)} %constant.80) | copy-start | bytes 147460
  33.7 0.8 %copy-start.7 = (pred[6,32,256]{2,1,0:T(32,128)(4,1)S(1)}, pred[6,32,256]{2,1,0:T(32,128)(4,1)}, u32[]{:S(2)}) copy-start(pred[6,32,256]{2,1,0:T(32,128)(4,1)} %constant.82) | copy-start | bytes 147460
  33.7 0.9 %copy-start.6 = (pred[6,32,256]{2,1,0:T(32,128)(4,1)S(1)}, pred[6,32,256]{2,1,0:T(32,128)(4,1)}, u32[]{:S(2)}) copy-start(pred[6,32,256]{2,1,0:T(32,128)(4,1)} %constant.81) | copy-start | bytes 147460
  34.6 0.9 %copy-start.3 = (f32[256,64]{1,0:T(8,128)S(1)}, f32[256,64]{1,0:T(8,128)}, u32[]{:S(2)}) copy-start(f32[256,64]{1,0:T(8,128)} %constant.56.clone) | copy-start | bytes 196612
  42.3 0.8 %copy-start.9 = (pred[18,4,512]{2,1,0:T(4,128)(4,1)S(1)}, pred[18,4,512]{2,1,0:T(4,128)(4,1)}, u32[]{:S(2)}) copy-start(pred[18,4,512]{2,1,0:T(4,128)(4,1)} %constant.77) | copy-start | bytes 110596
  42.3 0.8 %copy-start.10 = (pred[18,4,512]{2,1,0:T(4,128)(4,1)S(1)}, pred[18,4,512]{2,1,0:T(4,128)(4,1)}, u32[]{:S(2)}) copy-start(pred[18,4,512]{2,1,0:T(4,128)(4,1)} %constant.78) | copy-start | bytes 110596
  42.3 0.8 %copy-start.11 = (pred[18,4,512]{2,1,0:T(4,128)(4,1)S(1)}, pred[18,4,512]{2,1,0:T(4,128)(4,1)}, u32[]{:S(2)}) copy-start(pred[18,4,512]{2,1,0:T(4,128)(4,1)} %constant.79) | copy-start | bytes 110596
  43.1 1.0 %copy-start = (f32[512,32]{1,0:T(8,128)S(1)}, f32[512,32]{1,0:T(8,128)}, u32[]{:S(2)}) copy-start(f32[512,32]{1,0:T(8,128)} %constant.60.clone) | copy-start | bytes 196612
  43.1 30.4 %copy-start.2 = (f32[8,6,10,256]{3,0,2,1:T(8,128)S(1)}, f32[8,6,10,256]{3,0,2,1:T(8,128)}, u32[]{:S(2)}) copy-start(f32[8,6,10,256]{3,0,2,1:T(8,128)} %get-tuple-element.82) | copy-start | bytes 1474564
  73.8 3.0 %copy-start.18 = (bf16[2,4,1024]{2,1,0:T(4,128)(2,1)}, bf16[2,4,1024]{2,1,0:T(4,128)(2,1)S(1)}, u32[]{:S(2)}) copy-start(bf16[2,4,1024]{2,1,0:T(4,128)(2,1)S(1)} %constant_dynamic-update-slice_fusion) | copy-start | bytes 49156
